TPU v7x, 32 devices: a whole 2x2x4 slice. The times are simulated.
32 devices in a mesh: lat: 4 (over z), comp: 8 (over y, x, core).
Axes of the slice: x: 2, y: 2, z: 4, core: 2. Of those that a mesh axis runs over, the one named last changes fastest.
Arguments:
- spectrum: float32 [1152, 64, 512], P('comp', 'lat'), may hold values from 0.05 to 2
- mask: int32 [64, 512], replicated, may hold values 0 or 1
- courant: float32 [2, 1152], P(None, 'comp'), may hold values from -0.5 to 0.5
- proj_a: bfloat16 [1152, 1152], P('comp'), may hold values from -0.1875 to 0.1875
- proj_b: bfloat16 [1152, 1152], P('comp'), may hold values from -0.1875 to 0.1875
- proj_c: bfloat16 [1152, 1152], P('comp'), may hold values from -0.1875 to 0.1875
- proj_d: bfloat16 [1152, 1152], P('comp'), may hold values from -0.1875 to 0.1875
- stokes_kernel: float32 [1152, 64], replicated, may hold values from -0.1875 to 0.1875
- tile_points: int32 [4, 8, 2048], P('lat', 'comp'), may hold values from 0 to 8191
- tile_counts: int32 [4, 8], P('lat', 'comp'), may hold values from 1 to 2048, as said below
- tile_nbr: int32 [4, 8, 2, 2048], P('lat', 'comp'), may hold values from 0 to 2047, as said below
- vorticity: float32 [4, 8, 64, 2048], P('lat', 'comp'), may hold values from -6 to 6
- diffusivity: float32 [4, 8, 64, 2048], P('lat', 'comp'), may hold values from 0.1 to 1
Outputs:
- spectrum_out: float32 [1152, 64, 512], P('comp', 'lat')
- ocean_force: float32 [4, 8, 64, 2048], P('lat', 'comp')
Inputs may be any that keep to these rules, and one draw needn't show every extreme that they name: `mask`: 1 marks a sea cell, 0 land. `tile_counts`: in every latitude group some tile is full. `tile_nbr`: every entry is below its tile's count.
All inputs are finite; a program needn't handle non-finite values.
Results may differ from a plain program's by a relative error of at most 0.0033.
Values may be sent and summed in bfloat16 or wider, within the bound.
A program may use at most 128 MiB of HBM per device.

v0:
```python
import jax
import jax.numpy as jnp
from jax import lax
from jax.sharding import PartitionSpec as P

ADV = 2


time_step = 0.25


def with_halo(shard, sides, width):
    for axis, dim in sides:
        peers, length = (lax.axis_size(axis), shard.shape[dim])
        up = [(i, (i + 1) % peers) for i in range(peers - 1)]
        down = [(j, i) for i, j in up]
        last = lax.slice_in_dim(shard, length - width, length, axis=dim)
        leading = lax.slice_in_dim(shard, 0, width, axis=dim)
        before = lax.ppermute(last, axis, up)
        after = lax.ppermute(leading, axis, down)
        shard = jnp.concatenate([before, shard, after], axis=dim)
    return shard


def limiter(backward, forward):
    orient = jnp.sign(backward)
    bound = jnp.minimum(
        jnp.minimum(2.0 * jnp.abs(backward), orient * (backward + 2.0 * forward) / 3.0),
        2.0 * orient * forward,
    )
    return orient * jnp.maximum(bound, 0.0)


def face_flux(before, center, after, beyond, speed):
    plus_face = center + 0.5 * limiter(center - before, after - center)
    minus_face = after + 0.5 * limiter(after - beyond, center - after)
    return jnp.maximum(speed, 0.0) * plus_face + jnp.minimum(speed, 0.0) * minus_face


def lon_sweep(energy, speed, sea_part):
    flux = face_flux(
        jnp.roll(energy, 1, 2), energy, jnp.roll(energy, -1, 2), jnp.roll(energy, -2, 2), speed
    )
    return sea_part * (energy - (flux - jnp.roll(flux, 1, 2)))


def lat_sweep(padded, speed, sea_part):
    extent = padded.shape[1] - 4
    flux = face_flux(
        padded[:, 0 : extent + 1],
        padded[:, 1 : extent + 2],
        padded[:, 2 : extent + 3],
        padded[:, 3 : extent + 4],
        speed,
    )
    return sea_part * (padded[:, 2 : extent + 2] - (flux[:, 1:] - flux[:, :-1]))


def contract(weights, operand):
    return lax.dot_general(
        weights.astype(jnp.float32),
        operand,
        (((0,), (0,)), ((), ())),
        precision=lax.Precision.HIGHEST,
    )


def fold_with(operand, pieces):
    return (contract(pieces[0], operand), contract(pieces[1], operand))


def on_device(
    spectrum,
    mask,
    courant,
    proj_a,
    proj_b,
    proj_c,
    proj_d,
    stokes_kernel,
    tile_points,
    tile_counts,
    tile_nbr,
    vorticity,
    diffusivity,
):
    comp_count, row_count, lon_width = spectrum.shape
    band_index = lax.axis_index("lat")
    margin = 2 * ADV
    sea_mask = jnp.pad(mask.astype(jnp.float32), ((margin, margin), (0, 0)))
    beside_all = lax.dynamic_slice_in_dim(
        sea_mask, band_index * row_count, row_count + 2 * margin, 0
    )
    own_mask = beside_all[margin : margin + row_count]
    speed_lon = courant[0][:, None, None]
    speed_lat = courant[1][:, None, None]
    energy = spectrum * own_mask
    for substep in range(ADV):
        energy = lon_sweep(energy, speed_lon, own_mask)
        padded = with_halo(energy, (("lat", 1),), 2)
        energy = lat_sweep(padded, speed_lat, own_mask)
    flat = energy.reshape(comp_count, row_count * lon_width)
    points = lax.all_to_all(flat, "comp", split_axis=1, concat_axis=0, tiled=True)
    first, second = fold_with(
        points,
        (
            lax.all_gather(proj_a, "comp", axis=0, tiled=True),
            lax.all_gather(proj_b, "comp", axis=0, tiled=True),
        ),
    )
    product = first * second
    gain, loss = fold_with(
        product,
        (
            lax.all_gather(proj_c, "comp", axis=0, tiled=True),
            lax.all_gather(proj_d, "comp", axis=0, tiled=True),
        ),
    )
    updated = points + time_step * (gain - points * loss)
    profile = contract(stokes_kernel, updated).astype(jnp.bfloat16)
    group_profile = lax.all_gather(profile, "comp", axis=1, tiled=True)
    slots = jnp.take(group_profile, tile_points[0, 0], axis=1).astype(jnp.float32)
    live = (jnp.arange(slots.shape[1], dtype=jnp.int32) < tile_counts[0, 0]).astype(jnp.float32)
    east = jnp.take(slots, tile_nbr[0, 0, 0], axis=1)
    north = jnp.take(slots, tile_nbr[0, 0, 1], axis=1)
    upper = jnp.concatenate([slots[:1], slots[:-1]], axis=0)
    lower = jnp.concatenate([slots[1:], jnp.zeros_like(slots[:1])], axis=0)
    ocean_force = live[None, :] * (
        vorticity[0, 0] * (east - north) + diffusivity[0, 0] * (upper - 2.0 * slots + lower)
    )
    returned = lax.all_to_all(updated, "comp", split_axis=0, concat_axis=1, tiled=True)
    return (returned.reshape(comp_count, row_count, lon_width), ocean_force[None, None])


def solution(mesh):
    return jax.shard_map(
        on_device,
        mesh=mesh,
        in_specs=(
            P("comp", "lat", None),
            P(),
            P(None, "comp"),
            P("comp", None),
            P("comp", None),
            P("comp", None),
            P("comp", None),
            P(),
            P("lat", "comp", None),
            P("lat", "comp"),
            P("lat", "comp", None, None),
            P("lat", "comp", None, None),
            P("lat", "comp", None, None),
        ),
        out_specs=(P("comp", "lat", None), P("lat", "comp", None, None)),
        check_vma=False,
    )
```

profile of v0, /device:TPU:3, one launch (start us, length us, event | category | flops | bytes accessed | tf_op | source)
XLA Modules:
  0.0 420.1 jit_solution(7139510040805808831)
XLA Ops:
  8.9 5.1 %copy_multiply_fusion = f32[144,16,512]{2,0,1:T(8,128)S(1)} fusion(f32[144,16,512]{2,1,0:T(8,128)} %param.15, f32[16,512]{1,0:T(8,128)S(1)} %pad_dynamic-slice_fusion), kind=kLoop, calls=%fused_computation.50 | loop fusion | flops 1179648 | bytes 9469952 | tf_op jit(solution)/shard_map/mul | solution.py:97
  16.5 1.8 fusion.35
  18.4 5.4 %fusion.36 = (f32[144,16,511]{2,0,1:T(8,128)}, f32[144,16,511]{2,0,1:T(8,128)}) fusion(f32[144,16,512]{2,0,1:T(8,128)S(1)} %copy_multiply_fusion), kind=kLoop, calls=%fused_computation.86 | loop fusion | bytes 18837504 | tf_op jit(solution)/shard_map/jit(_roll_static)/slice | solution.py:42
  23.8 13.4 %multiply_add_fusion.3 = f32[144,16,512]{2,0,1:T(8,128)S(1)} fusion(f32[144,16,2]{2,0,1:T(8,128)} %slice.185, f32[144,16,510]{2,0,1:T(8,128)S(1)} %slice.184, f32[144,16,1]{2,0,1:T(8,128)} %get-tuple-element.20, f32[144,16,511]{2,0,1:T(8,128)} %get-tuple-element.22, f32[144,16,511]{2,0,1:T(8,128)} %get-tuple-element.21, f32[144,16,1]{2,0,1:T(8,128)} %get-tuple-element.19, ...), kind=kLoop, calls=%fused_computation.52 | loop fusion | flops 48365568 | bytes 23626880 | tf_op jit(solution)/shard_map/add | solution.py:37
  37.2 1.4 slice.186
  38.6 5.2 %fusion.15 = f32[144,16,512]{2,0,1:T(8,128)S(1)} fusion(f32[144,16,512]{2,0,1:T(8,128)S(1)} %multiply_add_fusion.3, f32[144,16,511]{2,0,1:T(8,128)S(1)} %bitcast.62, f32[144,16,1]{2,0,1:T(8,128)} %slice.186, f32[16,512]{1,0:T(8,128)S(1)} %pad_dynamic-slice_fusion, f32[144,16,512]{2,1,0:T(8,128)S(1)} %bitcast.68), kind=kLoop, calls=%fused_computation.39 | loop fusion | flops 5898240 | bytes 18907136 | tf_op jit(solution)/shard_map/mul | solution.py:44
  43.8 2.2 copy-done.2
  47.1 3.2 collective-permute-start
  50.4 1.3 collective-permute-start.1
  51.7 10.9 %collective-permute-done = f32[144,2,512]{2,0,1:T(8,128)S(1)} collective-permute-done((f32[144,2,512]{2,0,1:T(8,128)}, f32[144,2,512]{2,0,1:T(8,128)S(1)}, u32[]{:S(2)}, u32[]{:S(2)}) %collective-permute-start) | collective-permute-done | bytes 589856 | tf_op jit(solution)/shard_map/ppermute | solution.py:19
  62.6 3.9 collective-permute-done.1
  66.5 14.4 %multiply_add_fusion.1 = f32[144,17,512]{2,0,1:T(8,128)} fusion(f32[144,2,512]{2,0,1:T(8,128)S(1)} %collective-permute-done.1, f32[144,16,512]{2,0,1:T(8,128)} %copy-done.2, f32[144,2,512]{2,0,1:T(8,128)S(1)} %collective-permute-done, f32[144]{0:T(256)S(1)} %bitcast.78, f32[144]{0:T(256)S(1)} %bitcast.76), kind=kLoop, calls=%fused_computation.25 | loop fusion | flops 51388416 | bytes 10912896 | tf_op jit(solution)/shard_map/add | solution.py:37
  80.9 5.7 %fusion.13 = f32[144,16,512]{2,0,1:T(8,128)S(1)} fusion(f32[144,16,512]{2,0,1:T(8,128)S(1)} %bitcast.66, f32[144,17,512]{2,0,1:T(8,128)} %multiply_add_fusion.1, f32[16,512]{1,0:T(8,128)S(1)} %pad_dynamic-slice_fusion), kind=kLoop, calls=%fused_computation.33 | loop fusion | flops 3538944 | bytes 18907136 | tf_op jit(solution)/shard_map/mul | solution.py:56
  89.1 1.8 fusion.32
  91.0 3.9 fusion.33
  94.9 10.6 %multiply_add_fusion.2 = f32[144,16,512]{2,0,1:T(8,128)S(1)} fusion(f32[144,16,512]{2,0,1:T(8,128)S(1)} %fusion.13, f32[144,16,2]{2,0,1:T(8,128)} %slice.201, f32[144,16,510]{2,0,1:T(8,128)S(1)} %slice.200, f32[144,16,1]{2,0,1:T(8,128)} %get-tuple-element.14, f32[144,16,511]{2,0,1:T(8,128)} %get-tuple-element.16, f32[144,16,511]{2,0,1:T(8,128)S(1)} %get-tuple-element.15, ...), kind=kLoop, calls=%fused_computation.51 | loop fusion | flops 47185920 | bytes 23594112 | tf_op jit(solution)/shard_map/add | solution.py:37
  105.5 1.4 slice.202
  106.9 3.3 fusion.17
  110.2 2.2 copy-done.1
  113.6 3.2 collective-permute-start.2
  116.8 1.3 collective-permute-start.3
  118.1 10.8 %collective-permute-done.2 = f32[144,2,512]{2,0,1:T(8,128)S(1)} collective-permute-done((f32[144,2,512]{2,0,1:T(8,128)}, f32[144,2,512]{2,0,1:T(8,128)S(1)}, u32[]{:S(2)}, u32[]{:S(2)}) %collective-permute-start.2) | collective-permute-done | bytes 589856 | tf_op jit(solution)/shard_map/ppermute | solution.py:19
  128.9 3.9 collective-permute-done.3
  132.7 11.9 %multiply_add_fusion = f32[144,17,512]{2,0,1:T(8,128)S(1)} fusion(f32[144,2,512]{2,0,1:T(8,128)S(1)} %collective-permute-done.3, f32[144,16,512]{2,0,1:T(8,128)} %copy-done.1, f32[144,2,512]{2,0,1:T(8,128)S(1)} %collective-permute-done.2, f32[144]{0:T(256)S(1)} %bitcast.79, f32[144]{0:T(256)S(1)} %bitcast.77), kind=kLoop, calls=%fused_computation.23 | loop fusion | flops 51388416 | bytes 10912896 | tf_op jit(solution)/shard_map/add | solution.py:37
  146.0 4.9 %copy.38 = f32[144,16,512]{2,1,0:T(8,128)} copy(f32[144,16,512]{2,0,1:T(8,128)S(1)} %fusion.11) | data formatting | bytes 9437184 | tf_op jit(solution)/shard_map/mul | solution.py:56
  150.9 6.3 %all_to_all.26 = f32[144,8,1024]{2,1,0:T(8,128)} reshape(f32[144,16,512]{2,1,0:T(8,128)} %copy.38) | data formatting | bytes 9437184 | tf_op jit(solution)/shard_map/all_to_all | solution.py:103
  157.2 7.3 %copy.39 = f32[144,8,1024]{2,0,1:T(8,128)} copy(f32[144,8,1024]{2,1,0:T(8,128)} %all_to_all.26) | data formatting | bytes 9437184 | tf_op jit(solution)/shard_map/all_to_all | solution.py:103
  164.5 6.6 %all-to-all-start = ((f32[144,8,1024]{2,0,1:T(8,128)}), f32[144,8,1024]{2,0,1:T(8,128)}, u32[]{:S(2)}, u32[]{:S(2)}) async-start(f32[144,8,1024]{2,0,1:T(8,128)} %copy.39), calls=%async_computation | async-start | bytes 9437184 | tf_op jit(solution)/shard_map/all_to_all | solution.py:103
  171.6 63.4 %all-to-all-done = f32[144,8,1024]{2,0,1:T(8,128)} async-done(((f32[144,8,1024]{2,0,1:T(8,128)}), f32[144,8,1024]{2,0,1:T(8,128)}, u32[]{:S(2)}, u32[]{:S(2)}) %all-to-all-start) | async-done | bytes 4718624 | tf_op jit(solution)/shard_map/all_to_all | solution.py:103
  235.0 6.2 %copy.41 = f32[1152,1024]{0,1:T(8,128)} copy(f32[1152,1024]{1,0:T(8,128)} %bitcast.5) | data formatting | bytes 9437184 | tf_op jit(solution)/shard_map/all_to_all | solution.py:103
  241.2 14.3 %fusion.39 = f32[1024,1152]{1,0:T(8,128)} fusion(f32[1152,1024]{1,0:T(8,128)} %bitcast.5, bf16[1152,1152]{1,0:T(8,128)(2,1)} %all-gather.6.cloned.1.call-done), kind=kOutput, calls=%fused_computation.89 | convolution fusion | flops 16307453952 | bytes 12091392 | tf_op jit(solution)/shard_map/dot_general | solution.py:60
  255.6 15.1 %convolution_multiply_fusion = f32[1024,1152]{1,0:T(8,128)} fusion(f32[1024,1152]{1,0:T(8,128)} %fusion.39, f32[1152,1024]{1,0:T(8,128)} %bitcast.5, bf16[1152,1152]{1,0:T(8,128)(2,1)} %all-gather.8.cloned.1.call-done), kind=kOutput, calls=%fused_computation.27 | convolution fusion | flops 16308633600 | bytes 16809984 | tf_op jit(solution)/shard_map/dot_general | solution.py:60
  270.6 14.9 %fusion.40 = f32[1024,1152]{1,0:T(8,128)} fusion(f32[1024,1152]{1,0:T(8,128)} %convolution_multiply_fusion, bf16[1152,1152]{1,0:T(8,128)(2,1)} %all-gather.10.cloned.1.call-done), kind=kOutput, calls=%fused_computation.90 | convolution fusion | flops 16307453952 | bytes 12091392 | tf_op jit(solution)/shard_map/dot_general | solution.py:60
  285.5 17.2 %fusion.20 = f32[1152,1024]{0,1:T(8,128)} fusion(f32[1152,1024]{0,1:T(8,128)} %copy.41, f32[1024,1152]{1,0:T(8,128)} %fusion.40, f32[1024,1152]{1,0:T(8,128)} %convolution_multiply_fusion, bf16[1152,1152]{1,0:T(8,128)(2,1)} %all-gather.12.cloned.1.call-done), kind=kOutput, calls=%fused_computation.49 | convolution fusion | flops 16312172544 | bytes 21528576 | tf_op jit(solution)/shard_map/dot_general | solution.py:60
  302.7 6.1 %copy.42 = f32[1152,1024]{1,0:T(8,128)} copy(f32[1152,1024]{0,1:T(8,128)} %fusion.20) | data formatting | bytes 9437184 | tf_op jit(solution)/shard_map/add | solution.py:119
  308.8 6.2 %all-to-all-start.1 = ((f32[8,144,1024]{2,1,0:T(8,128)}), f32[8,144,1024]{2,1,0:T(8,128)}, u32[]{:S(2)}, u32[]{:S(2)}) async-start(f32[8,144,1024]{2,1,0:T(8,128)} %bitcast.69), calls=%async_computation.1 | async-start | bytes 9437184 | tf_op jit(solution)/shard_map/all_to_all | solution.py:131
  316.2 1.3 copy.46
  317.5 7.7 %fusion.21 = bf16[64,1024]{1,0:T(8,128)(2,1)} fusion(f32[1152,1024]{0,1:T(8,128)} %fusion.20, f32[1152,64]{0,1:T(8,128)S(1)} %copy-done), kind=kOutput, calls=%fused_computation.54 | convolution fusion | flops 906035200 | bytes 5144576 | tf_op jit(solution)/shard_map/dot_general | solution.py:60
  325.4 39.0 %all-gather.14.cloned.1.call-done = bf16[64,8192]{1,0:T(8,128)(2,1)} async-done(((bf16[64,1024]{1,0:T(8,128)(2,1)}), bf16[64,8192]{1,0:T(8,128)(2,1)}) %all-gather.14.cloned.1.call-update) | async-done | bytes 1048592 | tf_op jit(solution)/shard_map/all_gather | solution.py:121
  364.4 2.0 copy.45
  366.4 8.1 %gather_fusion = bf16[2048,64]{1,0:T(8,128)(2,1)} fusion(bf16[64,8192]{0,1:T(8,128)(2,1)S(1)} %copy.45, s32[2048]{0:T(1024)S(1)} %broadcast_clamp_fusion), kind=kCustom, calls=%fused_computation.2 | custom fusion | bytes 532480 | tf_op jit(solution)/shard_map/jit(_take)/gather | solution.py:122
  374.4 1.4 convert_bitcast_fusion
  375.8 7.6 %gather_fusion.1 = f32[2048,64]{1,0:T(8,128)} fusion(f32[64,2048]{0,1:T(8,128)S(1)} %convert_bitcast_fusion, s32[2048]{0:T(1024)S(1)} %fusion.29), kind=kCustom, calls=%fused_computation.clone | custom fusion | bytes 1056768 | tf_op jit(solution)/shard_map/jit(_take)/gather | solution.py:124
  383.5 7.6 %gather_fusion.2 = f32[2048,64]{1,0:T(8,128)} fusion(f32[64,2048]{0,1:T(8,128)S(1)} %convert_bitcast_fusion, s32[2048]{0:T(1024)S(1)} %fusion.30), kind=kCustom, calls=%fused_computation.1.clone | custom fusion | bytes 1056768 | tf_op jit(solution)/shard_map/jit(_take)/gather | solution.py:125
  392.6 5.2 %fusion.26 = f32[1,1,64,2048]{2,3,1,0:T(8,128)} fusion(f32[63,2048]{0,1:T(8,128)S(1)} %get-tuple-element.24, f32[1,2048]{0,1:T(8,128)S(1)} %bitcast.60, f32[1,1,64,2048]{2,3,1,0:T(8,128)S(1)} %copy-done.3, f32[1,1,64,2048]{2,3,1,0:T(8,128)S(1)} %copy.44, f32[2048,64]{1,0:T(8,128)S(1)} %copy-done.5, f32[2048,64]{1,0:T(8,128)S(1)} %copy-done.4, ...), kind=kLoop, calls=%fused_computation.60 | loop fusion | flops 1703936 | bytes 3938304 | tf_op jit(solution)/shard_map/broadcast_in_dim | solution.py:132
  397.8 2.3 copy.47
  400.2 7.2 %copy.43 = f32[144,8,1024]{2,1,0:T(8,128)} copy(f32[144,8,1024]{2,0,1:T(8,128)} %bitcast.10) | data formatting | bytes 9437184 | tf_op jit(solution)/shard_map/all_to_all | solution.py:131
  407.4 6.0 %reshape.97 = f32[144,16,512]{2,1,0:T(8,128)} reshape(f32[144,8,1024]{2,1,0:T(8,128)} %copy.43) | data formatting | bytes 9437184 | tf_op jit(solution)/shard_map/reshape | solution.py:132
  (69 shorter events, 13.2 us)
Async XLA Ops:
  7.2 310.4 %copy-start = (f32[1152,64]{0,1:T(8,128)S(1)}, f32[1152,64]{0,1:T(8,128)}, u32[]{:S(2)}) copy-start(f32[1152,64]{0,1:T(8,128)} %param.22) | copy-start | bytes 884740
  7.2 234.0 %all-gather.6.cloned.1.call-start = ((), (), s32[]{:S(2)}) async-start(), calls=%async_computation.2 | async-start | bytes 2985984 | tf_op jit(solution)/shard_map/all_gather | solution.py:107
  7.9 247.6 %all-gather.8.cloned.1.call-start = ((), (), s32[]{:S(2)}) async-start(), calls=%async_computation.3 | async-start | bytes 2985984 | tf_op jit(solution)/shard_map/all_gather | solution.py:108
  14.0 2.5 copy-start.10
  16.5 7.2 %slice-start.4 = ((s8[4718592]{0:T(1024)(128)(4,1)}), s8[4194304]{0:T(1024)(128)(4,1)S(1)}, s32[]{:S(2)}) async-start(s8[4718592]{0:T(1024)(128)(4,1)} %bitcast.67), calls=%async_computation.11 | async-start | bytes 8388608
  18.4 5.4 %slice-start.5 = ((s8[4718592]{0:T(1024)(128)(4,1)}), s8[524288]{0:T(1024)(128)(4,1)S(1)}, s32[]{:S(2)}) async-start(s8[4718592]{0:T(1024)(128)(4,1)} %bitcast.67), calls=%async_computation.12 | async-start | bytes 1048576
  43.8 2.2 copy-start.2
  47.1 15.5 %collective-permute-start = (f32[144,2,512]{2,0,1:T(8,128)}, f32[144,2,512]{2,0,1:T(8,128)S(1)}, u32[]{:S(2)}, u32[]{:S(2)}) collective-permute-start(f32[144,2,512]{2,0,1:T(8,128)} %get-tuple-element.17), channel_id=1, source_target_pairs={{0,8},{8,16},{16,24},{1,9},{9,17},{17,25},{2,10},{10,18},{18,26},{... | collective-permute-start | bytes 1769480 | tf_op jit(solution)/shard_map/ppermute | solution.py:19
  50.4 16.1 %collective-permute-start.1 = (f32[144,2,512]{2,0,1:T(8,128)}, f32[144,2,512]{2,0,1:T(8,128)S(1)}, u32[]{:S(2)}, u32[]{:S(2)}) collective-permute-start(f32[144,2,512]{2,0,1:T(8,128)} %get-tuple-element.18), channel_id=1, source_target_pairs={{8,0},{16,8},{24,16},{9,1},{17,9},{25,17},{10,2},{18,10},{26,18},{... | collective-permute-start | bytes 1769480 | tf_op jit(solution)/shard_map/ppermute | solution.py:20
  51.7 29.2 %slice-start.2 = ((s8[4718592]{0:T(1024)(128)(4,1)}), s8[524288]{0:T(1024)(128)(4,1)S(1)}, s32[]{:S(2)}) async-start(s8[4718592]{0:T(1024)(128)(4,1)} %bitcast.65), calls=%async_computation.9 | async-start | bytes 1048576
  51.7 218.9 %all-gather.10.cloned.1.call-start = ((), (), s32[]{:S(2)}) async-start(), calls=%async_computation.4 | async-start | bytes 2985984 | tf_op jit(solution)/shard_map/all_gather | solution.py:115
  66.5 14.4 %slice-start.3 = ((s8[4718592]{0:T(1024)(128)(4,1)}), s8[4194304]{0:T(1024)(128)(4,1)S(1)}, s32[]{:S(2)}) async-start(s8[4718592]{0:T(1024)(128)(4,1)} %bitcast.65), calls=%async_computation.10 | async-start | bytes 8388608
  110.2 2.2 copy-start.1
  113.6 15.3 %collective-permute-start.2 = (f32[144,2,512]{2,0,1:T(8,128)}, f32[144,2,512]{2,0,1:T(8,128)S(1)}, u32[]{:S(2)}, u32[]{:S(2)}) collective-permute-start(f32[144,2,512]{2,0,1:T(8,128)} %get-tuple-element.11), channel_id=1, source_target_pairs={{0,8},{8,16},{16,24},{1,9},{9,17},{17,25},{2,10},{10,18},{18,26},{... | collective-permute-start | bytes 1769480 | tf_op jit(solution)/shard_map/ppermute | solution.py:19
  116.8 16.0 %collective-permute-start.3 = (f32[144,2,512]{2,0,1:T(8,128)}, f32[144,2,512]{2,0,1:T(8,128)S(1)}, u32[]{:S(2)}, u32[]{:S(2)}) collective-permute-start(f32[144,2,512]{2,0,1:T(8,128)} %get-tuple-element.12), channel_id=1, source_target_pairs={{8,0},{16,8},{24,16},{9,1},{17,9},{25,17},{10,2},{18,10},{26,18},{... | collective-permute-start | bytes 1769480 | tf_op jit(solution)/shard_map/ppermute | solution.py:20
  118.1 26.6 %slice-start = ((s8[4718592]{0:T(1024)(128)(4,1)}), s8[524288]{0:T(1024)(128)(4,1)S(1)}, s32[]{:S(2)}) async-start(s8[4718592]{0:T(1024)(128)(4,1)} %bitcast.63), calls=%async_computation.7 | async-start | bytes 1048576
  118.1 26.6 %slice-start.1 = ((s8[4718592]{0:T(1024)(128)(4,1)}), s8[4194304]{0:T(1024)(128)(4,1)S(1)}, s32[]{:S(2)}) async-start(s8[4718592]{0:T(1024)(128)(4,1)} %bitcast.63), calls=%async_computation.8 | async-start | bytes 8388608
  164.5 70.5 %all-to-all-start = ((f32[144,8,1024]{2,0,1:T(8,128)}), f32[144,8,1024]{2,0,1:T(8,128)}, u32[]{:S(2)}, u32[]{:S(2)}) async-start(f32[144,8,1024]{2,0,1:T(8,128)} %copy.39), calls=%async_computation | async-start | bytes 9437184 | tf_op jit(solution)/shard_map/all_to_all | solution.py:103
  171.1 114.5 %all-gather.12.cloned.1.call-start = ((), (), s32[]{:S(2)}) async-start(), calls=%async_computation.5 | async-start | bytes 2985984 | tf_op jit(solution)/shard_map/all_gather | solution.py:116
  308.8 7.1 %copy-start.6 = (f32[1,1,64,2048]{3,2,1,0:T(8,128)S(1)}, f32[1,1,64,2048]{3,2,1,0:T(8,128)}, u32[]{:S(2)}) copy-start(f32[1,1,64,2048]{3,2,1,0:T(8,128)} %param.26) | copy-start | bytes 1572868
  308.8 7.5 %copy-start.7 = (f32[1,1,64,2048]{3,2,1,0:T(8,128)S(1)}, f32[1,1,64,2048]{3,2,1,0:T(8,128)}, u32[]{:S(2)}) copy-start(f32[1,1,64,2048]{3,2,1,0:T(8,128)} %param.27) | copy-start | bytes 1572868
  308.8 91.4 %all-to-all-start.1 = ((f32[8,144,1024]{2,1,0:T(8,128)}), f32[8,144,1024]{2,1,0:T(8,128)}, u32[]{:S(2)}, u32[]{:S(2)}) async-start(f32[8,144,1024]{2,1,0:T(8,128)} %bitcast.69), calls=%async_computation.1 | async-start | bytes 9437184 | tf_op jit(solution)/shard_map/all_to_all | solution.py:131
  315.0 10.3 %copy-start.8 = (s32[1,1,2048]{2,1,0:T(1,128)S(1)}, s32[1,1,2048]{2,1,0:T(1,128)}, u32[]{:S(2)}) copy-start(s32[1,1,2048]{2,1,0:T(1,128)} %param.23) | copy-start | bytes 24580
  315.0 10.3 %copy-start.9 = (s32[1,1,2,2048]{3,2,1,0:T(2,128)S(1)}, s32[1,1,2,2048]{3,2,1,0:T(2,128)}, u32[]{:S(2)}) copy-start(s32[1,1,2,2048]{3,2,1,0:T(2,128)} %param.25) | copy-start | bytes 49156
  315.0 49.4 %all-gather.14.cloned.1.call-start = ((), (), s32[]{:S(2)}) async-start(), calls=%async_computation.6 | async-start | bytes 1179648 | tf_op jit(solution)/shard_map/all_gather | solution.py:121
  383.4 8.0 %copy-start.3 = (f32[1,1,64,2048]{2,3,1,0:T(8,128)S(1)}, f32[1,1,64,2048]{2,3,1,0:T(8,128)}, u32[]{:S(2)}) copy-start(f32[1,1,64,2048]{2,3,1,0:T(8,128)} %copy.46) | copy-start | bytes 1572868
  391.1 1.2 copy-start.4
  391.1 1.5 copy-start.5
Sparse Core Ops, SparseCore 0:
  9.9 31.7 all-gather.5
  51.8 33.1 all-gather.7
  118.2 32.2 all-gather.9
  173.4 57.7 all-gather.11
  325.4 38.9 all-gather.13
where the time goes:
time: 427 us; the launch traced here: 420 us
  waiting for transfers between devices  133 us (31%)
  local copies, waits for them, and re-layouts  102 us (24%)
  other arithmetic  78.5 us (18%)
  matrix products  69.1 us (16%)
  starting transfers between devices  22.1 us (5%)
  between operations  14.9 us (3%)
    dot_general x5, matrix products, contract(): lax.dot_general(weights.astype(jnp.float32), operand, (((0,), (0,)), ((),...  69.1 us
    all_to_all x1, waiting for transfers between devices, on_device(): lax.all_to_all(flat, 'comp', split_axis=1, concat_axis=0, tiled=True)  63.4 us
    add x4, other arithmetic, face_flux(): jnp.maximum(speed, 0.0) * plus_face + jnp.minimum(speed, 0.0) * minus_face  50.4 us
    all_gather x1, waiting for transfers between devices, on_device(): group_profile = lax.all_gather(profile, 'comp', axis=1, tiled=True)  39 us
    ppermute x2, waiting for transfers between devices, with_halo(): before = lax.ppermute(last, axis, up)  21.6 us
    all_to_all x3, local copies, waits for them, and re-layouts, on_device(): lax.all_to_all(flat, 'comp', split_axis=1, concat_axis=0, tiled=True)  19.8 us
    slice x4, local copies, waits for them, and re-layouts, lon_sweep(): jnp.roll(energy, 1, 2)  13 us
    unnamed x37, local copies, waits for them, and re-layouts  9.6 us
  transfers between devices with their start and end apart: 11, of which 6 were waited for; matrix products, arithmetic and copies ran while one was open for 48% of the time, Pallas kernels for 0%

commit v1 on v0

v1 whole, which is shorter than its diff:
```python
import functools

import jax
import jax.numpy as jnp
from jax import lax
from jax.experimental import pallas as pl
from jax.experimental.pallas import tpu as pltpu
from jax.sharding import PartitionSpec as P

ADV = 2
time_step = 0.25
CB = 16
LANES = 128


def half_limited(b, f):
    t = b * (1.0 / 6.0) + f * (1.0 / 3.0)
    low = jnp.minimum(jnp.minimum(b, f), t)
    high = jnp.maximum(jnp.maximum(b, f), t)
    return jnp.maximum(low, 0.0) + jnp.minimum(high, 0.0)


def advect_kernel(rows, chunk, x_ref, up_ref, dn_ref, mask_ref, cour_ref, band_ref, e_ref, x_s):
    lon = x_ref.shape[1]
    cb = up_ref.shape[1]
    margin = 2 * ADV
    total = rows + 2 * margin
    c_lon = jnp.broadcast_to(cour_ref[:, 0:1], (cb, lon))
    c_lat = jnp.broadcast_to(cour_ref[:, 1:2], (cb, lon))
    a_lon, a_lat = jnp.abs(c_lon), jnp.abs(c_lat)
    pos_lon, pos_lat = c_lon > 0.0, c_lat > 0.0

    def lon_row(e, sea):
        nxt = pltpu.roll(e, lon - 1, 1)
        d = nxt - e
        b = jnp.where(pos_lon, pltpu.roll(d, 1, 1), pltpu.roll(d, lon - 1, 1))
        flux = c_lon * jnp.where(pos_lon, e, nxt) + a_lon * half_limited(b, d)
        return sea * (e - (flux - pltpu.roll(flux, 1, 1)))

    def sea_row(r):
        return mask_ref[pl.ds(r, 1), :]

    for j in range(lon // LANES):
        x_s[j] = x_ref[:, j * LANES : (j + 1) * LANES]

    for r in range(margin):
        sea = sea_row(r)
        e_ref[r] = lon_row(up_ref[r].astype(jnp.float32) * sea, sea)
        sea = sea_row(margin + rows + r)
        e_ref[margin + rows + r] = lon_row(dn_ref[r].astype(jnp.float32) * sea, sea)

    @pl.loop(0, rows)
    def _(r):
        sea = sea_row(margin + r)
        own = jnp.concatenate([x_s[j, pl.ds(r, cb, stride=rows), :] for j in range(lon // LANES)], axis=1)
        e_ref[margin + r] = lon_row(own * sea, sea)

    def face(e0, e1, dm, d, dp):
        b = jnp.where(pos_lat, dm, dp)
        return c_lat * jnp.where(pos_lat, e0, e1) + a_lat * half_limited(b, d)

    def lat_sweep(first, last, finish):
        em, e0, e1 = e_ref[first - 2], e_ref[first - 1], e_ref[first]
        e2 = e_ref[first + 1]
        d0 = e1 - e0
        d1 = e2 - e1
        flux = face(e0, e1, e0 - em, d0, d1)

        def step(r, carry):
            cur, nxt, dm, d, before = carry
            beyond = e_ref[r + 2]
            dp = beyond - nxt
            flux = face(cur, nxt, dm, d, dp)
            finish(r, cur - (flux - before), sea_row(r))
            return nxt, beyond, d, dp, flux

        lax.fori_loop(first, last, step, (e1, e2, d0, d1, flux))

    for substep in range(ADV):
        gone = 2 * (substep + 1)
        last_one = substep == ADV - 1

        def finish(r, value, sea):
            value = sea * value
            if not last_one:
                value = lon_row(value, sea)
            e_ref[r] = value

        lat_sweep(gone, total - gone, finish)
    dests = band_ref.shape[0]
    for d in range(dests):
        at = 0
        while at < chunk:
            point = d * chunk + at
            r, lane = point // lon, point % lon
            n = min(lon - lane, chunk - at)
            v = e_ref[margin + r][:, lane : lane + n]
            band_ref[d, :, at : at + n] = v
            at += n


def advect(spectrum, halo_up, halo_dn, mask_rows, cour, dests):
    comps, rows, lon = spectrum.shape
    chunk = rows * lon // dests
    margin = 2 * ADV
    total = rows + 2 * margin
    blk = pl.BlockSpec((dests, CB, chunk), lambda i: (0, i, 0))
    return pl.pallas_call(
        functools.partial(advect_kernel, rows, chunk),
        grid=(pl.cdiv(comps, CB),),
        in_specs=[
            pl.BlockSpec((CB * rows, lon), lambda i: (i, 0)),
            pl.BlockSpec((margin, CB, lon), lambda i: (0, i, 0)),
            pl.BlockSpec((margin, CB, lon), lambda i: (0, i, 0)),
            pl.BlockSpec((total, lon), lambda i: (0, 0)),
            pl.BlockSpec((CB, 2), lambda i: (i, 0)),
        ],
        out_specs=blk,
        out_shape=jax.ShapeDtypeStruct((dests, comps, chunk), jnp.float32),
        scratch_shapes=[
            pltpu.VMEM((total, CB, lon), jnp.float32),
            pltpu.VMEM((lon // LANES, CB * rows, LANES), jnp.float32),
        ],
        name="advect",
    )(spectrum.reshape(comps * rows, lon), halo_up, halo_dn, mask_rows, cour)


def finish_kernel(rows, band_ref, delta_ref, out_ref, o_s):
    dests, cb, chunk = band_ref.shape
    lon = out_ref.shape[1]
    for d in range(dests):
        at = 0
        while at < chunk:
            point = d * chunk + at
            r, lane = point // lon, point % lon
            n = min(lon - lane, chunk - at)
            v = band_ref[d, :, at : at + n] + delta_ref[d, :, at : at + n].astype(jnp.float32)
            for j in range(n // LANES):
                o_s[lane // LANES + j, pl.ds(r, cb, stride=rows), :] = v[:, j * LANES : (j + 1) * LANES]
            at += n
    for j in range(lon // LANES):
        out_ref[:, j * LANES : (j + 1) * LANES] = o_s[j]


def finish(band, delta, rows, lon):
    dests, comps, chunk = band.shape
    blk = pl.BlockSpec((dests, CB, chunk), lambda i: (0, i, 0))
    out = pl.pallas_call(
        functools.partial(finish_kernel, rows),
        grid=(pl.cdiv(comps, CB),),
        in_specs=[blk, blk],
        out_specs=pl.BlockSpec((CB * rows, lon), lambda i: (i, 0)),
        out_shape=jax.ShapeDtypeStruct((comps * rows, lon), jnp.float32),
        scratch_shapes=[pltpu.VMEM((lon // LANES, CB * rows, LANES), jnp.float32)],
        name="finish",
    )(band, delta)
    return out.reshape(comps, rows, lon)


NT = (((1,), (1,)), ((), ()))


def slots_kernel(prof_ref, pts_ref, out_ref):
    jb = pts_ref.shape[0]
    layers, points = prof_ref.shape
    step = min(512, points)
    pts = jnp.broadcast_to(pts_ref[...], (jb, step))
    lane = lax.broadcasted_iota(jnp.int32, (jb, step), 1)

    def body(k, acc):
        hot = jnp.where(pts - k * step == lane, 1.0, 0.0).astype(jnp.bfloat16)
        return acc + lax.dot_general(
            hot, prof_ref[:, pl.ds(pl.multiple_of(k * step, step), step)], NT, preferred_element_type=jnp.float32
        )

    acc = lax.fori_loop(0, points // step, body, jnp.zeros((jb, layers), jnp.float32))
    out_ref[...] = acc.astype(jnp.bfloat16)


def tile_kernel(all_ref, own_ref, east_ref, north_ref, live_ref, vort_ref, diff_ref, out_ref):
    jb = own_ref.shape[0]
    slots, layers = all_ref.shape
    step = min(512, slots)
    east = jnp.broadcast_to(east_ref[...], (jb, step))
    north = jnp.broadcast_to(north_ref[...], (jb, step))
    lane = lax.broadcasted_iota(jnp.int32, (jb, step), 1)

    def body(k, acc):
        one = jnp.where(east - k * step == lane, 1.0, 0.0)
        two = jnp.where(north - k * step == lane, 1.0, 0.0)
        rows = all_ref[pl.ds(pl.multiple_of(k * step, step), step), :]
        return acc + lax.dot_general(
            (one - two).astype(jnp.bfloat16), rows, (((1,), (0,)), ((), ())), preferred_element_type=jnp.float32
        )

    acc = lax.fori_loop(0, slots // step, body, jnp.zeros((jb, layers), jnp.float32))
    gap = acc.T
    s = own_ref[...].astype(jnp.float32).T
    upper = jnp.concatenate([s[:1], s[:-1]], axis=0)
    lower = jnp.concatenate([s[1:], jnp.zeros_like(s[:1])], axis=0)
    out_ref[...] = live_ref[...] * (vort_ref[...] * gap + diff_ref[...] * (upper - 2.0 * s + lower))


def ocean(profile, pts, count, nbr, vort, diff):
    layers, points = profile.shape
    slots = pts.shape[0]
    jb = min(256, slots)
    grid = (slots // jb,)
    picked = pl.pallas_call(
        slots_kernel,
        grid=grid,
        in_specs=[
            pl.BlockSpec((layers, points), lambda j: (0, 0)),
            pl.BlockSpec((jb, 1), lambda j: (j, 0)),
        ],
        out_specs=pl.BlockSpec((jb, layers), lambda j: (j, 0)),
        out_shape=jax.ShapeDtypeStruct((slots, layers), jnp.bfloat16),
        name="slots",
    )(profile, pts[:, None])
    live = (jnp.arange(slots, dtype=jnp.int32) < count).astype(jnp.float32)[None]
    col = pl.BlockSpec((jb, 1), lambda j: (j, 0))
    wide = pl.BlockSpec((layers, jb), lambda j: (0, j))
    return pl.pallas_call(
        tile_kernel,
        grid=grid,
        in_specs=[
            pl.BlockSpec((slots, layers), lambda j: (0, 0)),
            pl.BlockSpec((jb, layers), lambda j: (j, 0)),
            col,
            col,
            pl.BlockSpec((1, jb), lambda j: (0, j)),
            wide,
            wide,
        ],
        out_specs=wide,
        out_shape=jax.ShapeDtypeStruct((layers, slots), jnp.float32),
        name="tile",
    )(picked, picked, nbr[0][:, None], nbr[1][:, None], live, vort, diff)


def contract(weights, operand):
    return lax.dot_general(
        weights, operand, (((0,), (0,)), ((), ())), preferred_element_type=jnp.float32
    )


def on_device(
    spectrum,
    mask,
    courant,
    proj_a,
    proj_b,
    proj_c,
    proj_d,
    stokes_kernel,
    tile_points,
    tile_counts,
    tile_nbr,
    vorticity,
    diffusivity,
):
    comps, rows, lon = spectrum.shape
    margin = 2 * ADV
    bands, dests = lax.axis_size("lat"), lax.axis_size("comp")
    band_index = lax.axis_index("lat")
    sea = jnp.pad(mask.astype(jnp.float32), ((margin, margin), (0, 0)))
    mask_rows = lax.dynamic_slice_in_dim(sea, band_index * rows, rows + 2 * margin, 0)
    up = [(i, i + 1) for i in range(bands - 1)]
    down = [(j, i) for i, j in up]

    def edge(part):
        return part.astype(jnp.bfloat16).transpose(1, 0, 2)

    halo_up = lax.ppermute(edge(spectrum[:, rows - margin :]), "lat", up)
    halo_dn = lax.ppermute(edge(spectrum[:, :margin]), "lat", down)
    weights = [lax.all_gather(w, "comp", axis=0, tiled=True) for w in (proj_a, proj_b, proj_c, proj_d)]
    band = advect(spectrum, halo_up, halo_dn, mask_rows, courant.T, dests)
    points = lax.all_to_all(band.astype(jnp.float16), "comp", split_axis=0, concat_axis=0)
    chunk = points.shape[2]
    points = points.reshape(dests * comps, chunk)
    own = points.astype(jnp.float32)
    points = own.astype(jnp.bfloat16)
    product = (contract(weights[0], points) * contract(weights[1], points)).astype(jnp.bfloat16)
    delta = time_step * (contract(weights[2], product) - own * contract(weights[3], product))
    profile = lax.dot_general(
        stokes_kernel, own + delta, (((0,), (0,)), ((), ())), precision=lax.Precision.HIGHEST
    ).astype(jnp.bfloat16)
    group = lax.all_gather(profile, "comp", axis=1, tiled=True)
    back = lax.all_to_all(
        delta.astype(jnp.bfloat16).reshape(dests, comps, chunk), "comp", split_axis=0, concat_axis=0
    )
    force = ocean(group, tile_points[0, 0], tile_counts[0, 0], tile_nbr[0, 0], vorticity[0, 0], diffusivity[0, 0])
    return finish(band, back, rows, lon), force[None, None]


def solution(mesh):
    return jax.shard_map(
        on_device,
        mesh=mesh,
        in_specs=(
            P("comp", "lat", None),
            P(),
            P(None, "comp"),
            P("comp", None),
            P("comp", None),
            P("comp", None),
            P("comp", None),
            P(),
            P("lat", "comp", None),
            P("lat", "comp"),
            P("lat", "comp", None, None),
            P("lat", "comp", None, None),
            P("lat", "comp", None, None),
        ),
        out_specs=(P("comp", "lat", None), P("lat", "comp", None, None)),
        check_vma=False,
    )
```

time: 427 us -> 324 us (0.76); the launches traced: 420 us -> 322 us
  Pallas kernels: 0 us -> 152 us
  local copies, waits for them, and re-layouts: 102 us -> 21.6 us
  other arithmetic: 78.5 us -> 8.82 us
  waiting for transfers between devices: 133 us -> 67.9 us
  matrix products: 69.1 us -> 42.1 us
  starting transfers between devices: 22.1 us -> 15.2 us
    pallas_call x0 -> x4, Pallas kernels: none -> 152 us  [the longest x1 99.3 us: advect(): pl.pallas_call(functools.partial(advect_kernel, rows, chunk), grid=(pl.cd...]
    add x4 -> x0, other arithmetic: 50.4 us -> none  [face_flux(): jnp.maximum(speed, 0.0) * plus_face + jnp.minimum(speed, 0.0) * minus_face]
    all_to_all x2, waiting for transfers between devices: 63.4 us -> 30.9 us  [the longest x1 30.9 us: on_device(): lax.all_to_all(band.astype(jnp.float16), 'comp', split_axis=0, concat_axi...]
    all_to_all x4 -> x0, local copies, waits for them, and re-layouts: 27.1 us -> none  [the longest x3 19.8 us: on_device(): lax.all_to_all(flat, 'comp', split_axis=1, concat_axis=0, tiled=True)]
    dot_general x5, matrix products: 69.1 us -> 42.1 us  [the longest x4 32.9 us: contract(): lax.dot_general(weights, operand, (((0,), (0,)), ((), ())), preferred_ele...]
    slice x15 -> x0, local copies, waits for them, and re-layouts: 23.5 us -> none  [the longest x4 13 us: lon_sweep(): jnp.roll(energy, 1, 2)]
    gather x3 -> x0, local copies, waits for them, and re-layouts: 23.3 us -> none  [the longest x1 8.05 us: on_device(): jnp.take(group_profile, tile_points[0, 0], axis=1).astype(jnp.float32)]
    mul x5 -> x0, other arithmetic: 20.6 us -> none  [the longest x2 8.5 us: lon_sweep(): return sea_part * (energy - (flux - jnp.roll(flux, 1, 2)))]
  transfers between devices with their start and end apart: 11 -> 9, of which waited for: 6 -> 4; matrix products, arithmetic and copies ran while one was open for 48% -> 18% of each run, Pallas kernels for 0% -> 44%
where the time goes in v1:
time: 324 us; the launch traced here: 322 us
  Pallas kernels  152 us (47%)
  waiting for transfers between devices  67.9 us (21%)
  matrix products  42.1 us (13%)
  local copies, waits for them, and re-layouts  21.6 us (7%)
  starting transfers between devices  15.2 us (5%)
  between operations  14.6 us (5%)
  other arithmetic  8.82 us (3%)
    pallas_call x1, Pallas kernels, advect(): pl.pallas_call(functools.partial(advect_kernel, rows, chunk), grid=(pl.cd...  99.3 us
    dot_general x4, matrix products, contract(): lax.dot_general(weights, operand, (((0,), (0,)), ((), ())), preferred_ele...  32.9 us
    pallas_call x1, Pallas kernels, ocean(): pl.pallas_call(slots_kernel, grid=grid, in_specs=[pl.BlockSpec((layers, p...  30.9 us
    all_to_all x1, waiting for transfers between devices, on_device(): lax.all_to_all(band.astype(jnp.float16), 'comp', split_axis=0, concat_axi...  30.9 us
    all_gather x1, waiting for transfers between devices, on_device(): group = lax.all_gather(profile, 'comp', axis=1, tiled=True)  21.2 us
    pallas_call x1, Pallas kernels, ocean(): pl.pallas_call(tile_kernel, grid=grid, in_specs=[pl.BlockSpec((slots, lay...  12.5 us
    ppermute x1, waiting for transfers between devices, on_device(): halo_up = lax.ppermute(edge(spectrum[:, rows - margin:]), 'lat', up)  9.23 us
    dot_general x1, matrix products, on_device(): lax.dot_general(stokes_kernel, own + delta, (((0,), (0,)), ((), ())), pre...  9.17 us
  transfers between devices with their start and end apart: 9, of which 4 were waited for; matrix products, arithmetic and copies ran while one was open for 18% of the time, Pallas kernels for 44%

profile of v1, /device:TPU:3, one launch (start us, length us, event | category | flops | bytes accessed | tf_op | source)
XLA Modules:
  0.0 322.0 jit_solution(4120920069898949327)
XLA Ops:
  7.2 0.0 copy-start
  7.2 0.0 all-gather.6.cloned.1.call-start
  7.2 0.7 all-gather.6.cloned.1.call-update
  7.9 0.0 all-gather.8.cloned.1.call-start
  8.0 0.7 all-gather.8.cloned.1.call-update
  8.7 0.0 all-gather.10.cloned.1.call-start
  8.7 0.7 all-gather.10.cloned.1.call-update
  9.4 0.0 copy-start.6
  9.4 4.9 %copy.29 = bf16[144,16,512]{2,0,1:T(8,128)(2,1)S(1)} copy(f32[144,16,512]{2,1,0:T(8,128)} %param.13) | data formatting | bytes 7077888 | tf_op args[0]
  14.3 0.1 slice_bitcast_fusion
  14.4 3.2 %collective-permute-start = (bf16[4,144,512]{2,1,0:T(8,128)(2,1)S(1)}, bf16[4,144,512]{2,1,0:T(8,128)(2,1)S(1)}, u32[]{:S(2)}, u32[]{:S(2)}) collective-permute-start(bf16[4,144,512]{2,1,0:T(8,128)(2,1)S(1)} %get-tuple-element.5), channel_id=1, source_target_pairs={{0,8},{8,16},{16,24},{1,9},{9,17},{17,25},{2,10},{10,18},{18,26},{... | collective-permute-start | bytes 1769480 | tf_op jit(solution)/shard_map/ppermute | solution.py:274
  17.7 1.3 collective-permute-start.1
  19.0 0.7 copy.21
  19.7 0.6 pad_dynamic-slice_fusion.mask_ref
  20.4 9.2 %collective-permute-done.up_ref = bf16[4,144,512]{2,1,0:T(8,128)(2,1)S(1)} collective-permute-done((bf16[4,144,512]{2,1,0:T(8,128)(2,1)S(1)}, bf16[4,144,512]{2,1,0:T(8,128)(2,1)S(1)}, u32[]{:S(2)}, u32[]{:S(2)}) %collective-permute-start) | collective-permute-done | bytes 589856 | tf_op jit(solution)/shard_map/ppermute | solution.py:274
  29.6 4.0 %collective-permute-done.1.dn_ref = bf16[4,144,512]{2,1,0:T(8,128)(2,1)S(1)} collective-permute-done((bf16[4,144,512]{2,1,0:T(8,128)(2,1)S(1)}, bf16[4,144,512]{2,1,0:T(8,128)(2,1)S(1)}, u32[]{:S(2)}, u32[]{:S(2)}) %collective-permute-start.1) | collective-permute-done | bytes 589856 | tf_op jit(solution)/shard_map/ppermute | solution.py:275
  33.6 0.8 copy-done.5
  34.4 99.3 %advect.1.band_ref = f32[8,144,1024]{2,1,0:T(8,128)} custom-call(f32[2304,512]{1,0:T(8,128)} %bitcast.42, bf16[4,144,512]{2,1,0:T(8,128)(2,1)} %copy-done.4, bf16[4,144,512]{2,1,0:T(8,128)(2,1)} %copy-done.5, f32[24,512]{1,0:T(8,128)} %pad_dynamic-slice_fusion.mask_ref, f32[144,2]{1,0:T(8,128)} %bitcast.48), custom_call_target="tpu_custom_call" | custom-call | tf_op jit(solution)/shard_map/advect/pallas_call | solution.py:108
  133.8 4.2 %convert_element_type.43 = f16[8,144,1024]{2,1,0:T(8,128)(2,1)} convert(f32[8,144,1024]{2,1,0:T(8,128)} %advect.1.band_ref) | non-fusion elementwise | flops 1179648 | bytes 7077888 | tf_op jit(solution)/shard_map/convert_element_type | solution.py:278
  138.0 5.5 %all-to-all-start = ((f16[8,144,1024]{2,1,0:T(8,128)(2,1)}), f16[8,144,1024]{2,1,0:T(8,128)(2,1)S(1)}, u32[]{:S(2)}, u32[]{:S(2)}) async-start(f16[8,144,1024]{2,1,0:T(8,128)(2,1)} %convert_element_type.43), calls=%async_computation | async-start | bytes 4718592 | tf_op jit(solution)/shard_map/all_to_all | solution.py:278
  143.5 0.0 all-gather.12.cloned.1.call-start
  143.5 0.6 all-gather.12.cloned.1.call-update
  144.1 30.9 %all-to-all-done = f16[8,144,1024]{2,1,0:T(8,128)(2,1)S(1)} async-done(((f16[8,144,1024]{2,1,0:T(8,128)(2,1)}), f16[8,144,1024]{2,1,0:T(8,128)(2,1)S(1)}, u32[]{:S(2)}, u32[]{:S(2)}) %all-to-all-start) | async-done | bytes 2359328 | tf_op jit(solution)/shard_map/all_to_all | solution.py:278
  174.9 4.0 %fusion.5 = (bf16[1152,1024]{1,0:T(8,128)(2,1)}, f32[1152,1024]{1,0:T(8,128)}) fusion(f16[8,144,1024]{2,1,0:T(8,128)(2,1)S(1)} %all-to-all-done), kind=kLoop, calls=%fused_computation.9 | loop fusion | flops 2359296 | bytes 9437184 | tf_op jit(solution)/shard_map/convert_element_type | solution.py:282
  178.9 6.3 %copy.22 = f32[1152,1024]{0,1:T(8,128)} copy(f32[1152,1024]{1,0:T(8,128)} %get-tuple-element.3) | data formatting | bytes 9437184 | tf_op jit(solution)/shard_map/convert_element_type | solution.py:281
  185.2 7.0 %fusion.13 = f32[1024,1152]{1,0:T(8,128)} fusion(bf16[1152,1024]{1,0:T(8,128)(2,1)S(1)} %copy-done.3, bf16[1152,1152]{1,0:T(8,128)(2,1)} %all-gather.6.cloned.1.call-done), kind=kOutput, calls=%fused_computation.19 | convolution fusion | flops 2717908992 | bytes 9732096 | tf_op jit(solution)/shard_map/dot_general | solution.py:242
  192.2 7.4 %fusion.4 = bf16[1024,1152]{1,0:T(8,128)(2,1)S(1)} fusion(f32[1024,1152]{1,0:T(8,128)} %fusion.13, bf16[1152,1024]{1,0:T(8,128)(2,1)} %get-tuple-element.2, bf16[1152,1152]{1,0:T(8,128)(2,1)} %all-gather.8.cloned.1.call-done), kind=kOutput, calls=%fused_computation.7 | convolution fusion | flops 2720268288 | bytes 12091392 | tf_op jit(solution)/shard_map/dot_general | solution.py:242
  199.6 0.0 all-gather.10.cloned.1.call-done
  199.6 7.7 %fusion.14 = f32[1024,1152]{1,0:T(8,128)} fusion(bf16[1024,1152]{1,0:T(8,128)(2,1)S(1)} %fusion.4, bf16[1152,1152]{1,0:T(8,128)(2,1)} %all-gather.10.cloned.1.call-done), kind=kOutput, calls=%fused_computation.20 | convolution fusion | flops 2717908992 | bytes 9732096 | tf_op jit(solution)/shard_map/dot_general | solution.py:242
  207.3 10.9 %fusion.12 = (bf16[1152,1024]{0,1:T(8,128)(2,1)S(1)}, f32[1152,1024]{0,1:T(8,128)}) fusion(f32[1152,1024]{0,1:T(8,128)} %copy.22, bf16[1024,1152]{1,0:T(8,128)(2,1)} %copy-done.2, bf16[1152,1152]{1,0:T(8,128)(2,1)} %all-gather.12.cloned.1.call-done, f32[1024,1152]{1,0:T(8,128)} %fusion.14), kind=kOutput, calls=%fused_computation.18 | convolution fusion | flops 2722627584 | bytes 21528576 | tf_op jit(solution)/shard_map/dot_general | solution.py:242
  218.2 2.5 copy.23
  220.7 5.1 %all-to-all-start.1 = ((bf16[8,144,1024]{2,1,0:T(8,128)(2,1)}), bf16[8,144,1024]{2,1,0:T(8,128)(2,1)S(1)}, u32[]{:S(2)}, u32[]{:S(2)}) async-start(bf16[8,144,1024]{2,1,0:T(8,128)(2,1)} %bitcast.43), calls=%async_computation.1 | async-start | bytes 4718592 | tf_op jit(solution)/shard_map/all_to_all | solution.py:289
  225.7 0.0 all-gather.14.cloned.1.call-start
  225.8 0.0 copy-done
  225.8 0.0 copy-start.8
  225.8 0.0 copy-start.7
  225.8 9.2 %fusion.9 = bf16[64,1024]{1,0:T(8,128)(2,1)} fusion(f32[1152,64]{0,1:T(8,128)S(1)} %copy-done, f32[1152,1024]{0,1:T(8,128)} %copy.22, f32[1152,1024]{0,1:T(8,128)} %get-tuple-element.9), kind=kOutput, calls=%fused_computation.11 | convolution fusion | flops 907214848 | bytes 9863168 | tf_op jit(solution)/shard_map/dot_general | solution.py:285
  235.0 0.0 all-gather.14.cloned.1.call-update
  235.0 1.3 copy.25.pts_ref
  236.4 1.4 copy.26.east_ref
  237.7 1.4 copy.27.north_ref
  239.7 0.6 compare_convert_fusion.live_ref
  240.4 21.2 %all-gather.14.cloned.1.call-done.prof_ref = bf16[64,8192]{1,0:T(8,128)(2,1)} async-done(((bf16[64,1024]{1,0:T(8,128)(2,1)}), bf16[64,8192]{1,0:T(8,128)(2,1)}) %all-gather.14.cloned.1.call-update) | async-done | bytes 1048592 | tf_op jit(solution)/shard_map/all_gather | solution.py:288
  261.5 30.9 %slots.1.all_ref.own_ref = bf16[2048,64]{1,0:T(8,128)(2,1)} custom-call(bf16[64,8192]{1,0:T(8,128)(2,1)} %all-gather.14.cloned.1.call-done.prof_ref, s32[2048,1]{1,0:T(8,128)} %copy.25.pts_ref), custom_call_target="tpu_custom_call" | custom-call | tf_op jit(solution)/shard_map/slots/pallas_call | solution.py:209
  292.5 12.5 %tile.1 = f32[64,2048]{1,0:T(8,128)} custom-call(bf16[2048,64]{1,0:T(8,128)(2,1)} %slots.1.all_ref.own_ref, bf16[2048,64]{1,0:T(8,128)(2,1)} %slots.1.all_ref.own_ref, s32[2048,1]{1,0:T(8,128)} %copy.26.east_ref, s32[2048,1]{1,0:T(8,128)} %copy.27.north_ref, f32[1,2048]{1,0:T(1,128)} %compare_convert_fusion.live_ref, f32[64,2048]{1,0:T(8,128)} %bitcast.45, ...), custom_call_target="tpu_custom_call" | custom-call | tf_op jit(solution)/shard_map/tile/pallas_call | solution.py:223
  305.0 0.0 all-to-all-done.1.delta_ref
  305.0 1.4 copy-done.1
  306.4 9.1 %finish.1 = f32[2304,512]{1,0:T(8,128)} custom-call(f32[8,144,1024]{2,1,0:T(8,128)} %advect.1.band_ref, bf16[8,144,1024]{2,1,0:T(8,128)(2,1)} %copy-done.1), custom_call_target="tpu_custom_call" | custom-call | tf_op jit(solution)/shard_map/finish/pallas_call | solution.py:148
  (18 shorter events, 0.1 us)
Async XLA Ops:
  7.2 218.6 %copy-start = (f32[1152,64]{0,1:T(8,128)S(1)}, f32[1152,64]{0,1:T(8,128)}, u32[]{:S(2)}) copy-start(f32[1152,64]{0,1:T(8,128)} %param.20) | copy-start | bytes 884740
  7.2 178.0 %all-gather.6.cloned.1.call-start = ((), (), s32[]{:S(2)}) async-start(), calls=%async_computation.2 | async-start | bytes 2985984 | tf_op jit(solution)/shard_map/all_gather | solution.py:276
  7.9 184.3 %all-gather.8.cloned.1.call-start = ((), (), s32[]{:S(2)}) async-start(), calls=%async_computation.3 | async-start | bytes 2985984 | tf_op jit(solution)/shard_map/all_gather | solution.py:276
  8.7 191.0 %all-gather.10.cloned.1.call-start = ((), (), s32[]{:S(2)}) async-start(), calls=%async_computation.4 | async-start | bytes 2985984 | tf_op jit(solution)/shard_map/all_gather | solution.py:276
  9.4 9.6 %copy-start.6 = (s32[64,512]{1,0:T(8,128)S(1)}, s32[64,512]{1,0:T(8,128)}, u32[]{:S(2)}) copy-start(s32[64,512]{1,0:T(8,128)} %param.14) | copy-start | bytes 393220
  9.4 9.6 %copy-start.9 = (f32[2,144]{1,0:T(2,128)S(1)}, f32[2,144]{1,0:T(2,128)}, u32[]{:S(2)}) copy-start(f32[2,144]{1,0:T(2,128)} %param.15) | copy-start | bytes 3460
  14.4 15.2 %collective-permute-start = (bf16[4,144,512]{2,1,0:T(8,128)(2,1)S(1)}, bf16[4,144,512]{2,1,0:T(8,128)(2,1)S(1)}, u32[]{:S(2)}, u32[]{:S(2)}) collective-permute-start(bf16[4,144,512]{2,1,0:T(8,128)(2,1)S(1)} %get-tuple-element.5), channel_id=1, source_target_pairs={{0,8},{8,16},{16,24},{1,9},{9,17},{17,25},{2,10},{10,18},{18,26},{... | collective-permute-start | bytes 1769480 | tf_op jit(solution)/shard_map/ppermute | solution.py:274
  17.7 15.9 %collective-permute-start.1 = (bf16[4,144,512]{2,1,0:T(8,128)(2,1)S(1)}, bf16[4,144,512]{2,1,0:T(8,128)(2,1)S(1)}, u32[]{:S(2)}, u32[]{:S(2)}) collective-permute-start(bf16[4,144,512]{2,1,0:T(8,128)(2,1)S(1)} %get-tuple-element.4), channel_id=1, source_target_pairs={{8,0},{16,8},{24,16},{9,1},{17,9},{25,17},{10,2},{18,10},{26,18},{... | collective-permute-start | bytes 1769480 | tf_op jit(solution)/shard_map/ppermute | solution.py:275
  29.6 4.0 %copy-start.4 = (bf16[4,144,512]{2,1,0:T(8,128)(2,1)}, bf16[4,144,512]{2,1,0:T(8,128)(2,1)S(1)}, u32[]{:S(2)}) copy-start(bf16[4,144,512]{2,1,0:T(8,128)(2,1)S(1)} %collective-permute-done.up_ref) | copy-start | bytes 1769476
  33.6 0.8 copy-start.5
  138.0 37.0 %all-to-all-start = ((f16[8,144,1024]{2,1,0:T(8,128)(2,1)}), f16[8,144,1024]{2,1,0:T(8,128)(2,1)S(1)}, u32[]{:S(2)}, u32[]{:S(2)}) async-start(f16[8,144,1024]{2,1,0:T(8,128)(2,1)} %convert_element_type.43), calls=%async_computation | async-start | bytes 4718592 | tf_op jit(solution)/shard_map/all_to_all | solution.py:278
  143.5 63.8 %all-gather.12.cloned.1.call-start = ((), (), s32[]{:S(2)}) async-start(), calls=%async_computation.5 | async-start | bytes 2985984 | tf_op jit(solution)/shard_map/all_gather | solution.py:276
  178.9 6.3 %copy-start.3 = (bf16[1152,1024]{1,0:T(8,128)(2,1)S(1)}, bf16[1152,1024]{1,0:T(8,128)(2,1)}, u32[]{:S(2)}) copy-start(bf16[1152,1024]{1,0:T(8,128)(2,1)} %get-tuple-element.2) | copy-start | bytes 7077892
  199.6 7.7 %copy-start.2 = (bf16[1024,1152]{1,0:T(8,128)(2,1)}, bf16[1024,1152]{1,0:T(8,128)(2,1)S(1)}, u32[]{:S(2)}) copy-start(bf16[1024,1152]{1,0:T(8,128)(2,1)S(1)} %fusion.4) | copy-start | bytes 7077892
  220.7 84.3 %all-to-all-start.1 = ((bf16[8,144,1024]{2,1,0:T(8,128)(2,1)}), bf16[8,144,1024]{2,1,0:T(8,128)(2,1)S(1)}, u32[]{:S(2)}, u32[]{:S(2)}) async-start(bf16[8,144,1024]{2,1,0:T(8,128)(2,1)} %bitcast.43), calls=%async_computation.1 | async-start | bytes 4718592 | tf_op jit(solution)/shard_map/all_to_all | solution.py:289
  225.7 35.8 %all-gather.14.cloned.1.call-start = ((), (), s32[]{:S(2)}) async-start(), calls=%async_computation.6 | async-start | bytes 1179648 | tf_op jit(solution)/shard_map/all_gather | solution.py:288
  225.8 9.2 %copy-start.8 = (s32[1,1,2048]{2,1,0:T(1,128)S(1)}, s32[1,1,2048]{2,1,0:T(1,128)}, u32[]{:S(2)}) copy-start(s32[1,1,2048]{2,1,0:T(1,128)} %param.21) | copy-start | bytes 24580
  225.8 10.6 %copy-start.7 = (s32[1,1,2,2048]{3,2,1,0:T(2,128)S(1)}, s32[1,1,2,2048]{3,2,1,0:T(2,128)}, u32[]{:S(2)}) copy-start(s32[1,1,2,2048]{3,2,1,0:T(2,128)} %param.23) | copy-start | bytes 49156
  305.0 1.5 copy-start.1
Sparse Core Ops, SparseCore 0:
  9.9 31.8 all-gather.5
  43.6 30.5 all-gather.7
  76.0 30.5 all-gather.9
  145.9 40.3 all-gather.11
  235.1 26.3 all-gather.13

commit v2 on v1

v2 whole, which is shorter than its diff:
```python
import functools

import jax
import jax.numpy as jnp
from jax import lax
from jax.experimental import pallas as pl
from jax.experimental.pallas import tpu as pltpu
from jax.sharding import PartitionSpec as P

ADV = 2
time_step = 0.25
CB = 16
LANES = 128
LOW = 256


def half_limited(b, f):
    t = b * (1.0 / 6.0) + f * (1.0 / 3.0)
    low = jnp.minimum(jnp.minimum(b, f), t)
    high = jnp.maximum(jnp.maximum(b, f), t)
    return jnp.maximum(low, 0.0) + jnp.minimum(high, 0.0)


def advect_kernel(rows, chunk, x_ref, up_ref, dn_ref, mask_ref, cour_ref, band_ref, a_s, b_s, u_s, x_s):
    lon = x_ref.shape[1]
    margin = 2 * ADV
    total = rows + 2 * margin
    dests = band_ref.shape[0]
    for j in range(lon // LANES):
        x_s[j] = x_ref[:, j * LANES : (j + 1) * LANES]
    for r in range(margin):
        u_s[r] = up_ref[r].astype(jnp.float32)
        u_s[margin + r] = dn_ref[r].astype(jnp.float32)

    def wide(column):
        return jnp.concatenate([jnp.broadcast_to(column, (8, LANES))] * (lon // LANES), axis=1)

    @pl.loop(0, CB // 8)
    def _(half):
        base = pl.multiple_of(half * 8, 8)
        cour = cour_ref[pl.ds(base, 8), :]
        c_lon, c_lat = wide(cour[:, 0:1]), wide(cour[:, 1:2])
        a_lon, a_lat = jnp.abs(c_lon), jnp.abs(c_lat)
        pos_lon, pos_lat = c_lon > 0.0, c_lat > 0.0

        def sea_row(r):
            return mask_ref[r : r + 1, :]

        def lon_row(e, sea):
            nxt = pltpu.roll(e, lon - 1, 1)
            d = nxt - e
            b = jnp.where(pos_lon, pltpu.roll(d, 1, 1), pltpu.roll(d, lon - 1, 1))
            flux = c_lon * jnp.where(pos_lon, e, nxt) + a_lon * half_limited(b, d)
            return sea * (e - (flux - pltpu.roll(flux, 1, 1)))

        def start_row(r):
            if r < margin:
                return u_s[r, pl.ds(base, 8), :]
            if r >= margin + rows:
                return u_s[r - rows, pl.ds(base, 8), :]
            first = half * (8 * rows) + (r - margin)
            return jnp.concatenate(
                [x_s[j, pl.ds(first, 8, stride=rows), :] for j in range(lon // LANES)], axis=1
            )

        def store_row(r, value):
            at = 0
            while at < lon:
                d, lane = divmod((r - margin) * lon + at, chunk)
                n = min(chunk - lane, lon - at)
                band_ref[d, pl.ds(base, 8), lane : lane + n] = value[:, at : at + n]
                at += n

        for substep in range(ADV):
            gone = 2 * substep
            for r in range(gone, total - gone):
                sea = sea_row(r)
                e = start_row(r) * sea if substep == 0 else b_s[r]
                a_s[r] = lon_row(e, sea)
            cur, nxt = a_s[gone], a_s[gone + 1]
            d = nxt - cur
            dm, before = d, None
            for r in range(gone + 1, total - gone - 2):
                cur, nxt, dm = nxt, a_s[r + 1], d
                d = nxt - cur
                dp = a_s[r + 2] - nxt
                b = jnp.where(pos_lat, dm, dp)
                flux = c_lat * jnp.where(pos_lat, cur, nxt) + a_lat * half_limited(b, d)
                if before is not None:
                    value = sea_row(r) * (cur - (flux - before))
                    if substep == ADV - 1:
                        store_row(r, value)
                    else:
                        b_s[r] = value
                before = flux


def advect(spectrum, halo_up, halo_dn, mask_rows, cour, dests):
    comps, rows, lon = spectrum.shape
    chunk = rows * lon // dests
    margin = 2 * ADV
    total = rows + 2 * margin
    blk = pl.BlockSpec((dests, CB, chunk), lambda i: (0, i, 0))
    return pl.pallas_call(
        functools.partial(advect_kernel, rows, chunk),
        grid=(pl.cdiv(comps, CB),),
        in_specs=[
            pl.BlockSpec((CB * rows, lon), lambda i: (i, 0)),
            pl.BlockSpec((margin, CB, lon), lambda i: (0, i, 0)),
            pl.BlockSpec((margin, CB, lon), lambda i: (0, i, 0)),
            pl.BlockSpec((total, lon), lambda i: (0, 0)),
            pl.BlockSpec((CB, 2), lambda i: (i, 0)),
        ],
        out_specs=blk,
        out_shape=jax.ShapeDtypeStruct((dests, comps, chunk), jnp.float32),
        scratch_shapes=[
            pltpu.VMEM((total, 8, lon), jnp.float32),
            pltpu.VMEM((total, 8, lon), jnp.float32),
            pltpu.VMEM((2 * margin, CB, lon), jnp.float32),
            pltpu.VMEM((lon // LANES, CB * rows, LANES), jnp.float32),
        ],
        name="advect",
    )(spectrum.reshape(comps * rows, lon), halo_up, halo_dn, mask_rows, cour)


def finish_kernel(rows, band_ref, delta_ref, out_ref, o_s):
    dests, cb, chunk = band_ref.shape
    lon = out_ref.shape[1]
    for d in range(dests):
        at = 0
        while at < chunk:
            point = d * chunk + at
            r, lane = point // lon, point % lon
            n = min(lon - lane, chunk - at)
            v = band_ref[d, :, at : at + n] + delta_ref[d, :, at : at + n].astype(jnp.float32)
            for j in range(n // LANES):
                o_s[lane // LANES + j, pl.ds(r, cb, stride=rows), :] = v[:, j * LANES : (j + 1) * LANES]
            at += n
    for j in range(lon // LANES):
        out_ref[:, j * LANES : (j + 1) * LANES] = o_s[j]


def finish(band, delta, rows, lon):
    dests, comps, chunk = band.shape
    blk = pl.BlockSpec((dests, CB, chunk), lambda i: (0, i, 0))
    out = pl.pallas_call(
        functools.partial(finish_kernel, rows),
        grid=(pl.cdiv(comps, CB),),
        in_specs=[blk, blk],
        out_specs=pl.BlockSpec((CB * rows, lon), lambda i: (i, 0)),
        out_shape=jax.ShapeDtypeStruct((comps * rows, lon), jnp.float32),
        scratch_shapes=[pltpu.VMEM((lon // LANES, CB * rows, LANES), jnp.float32)],
        name="finish",
    )(band, delta)
    return out.reshape(comps, rows, lon)


NT = (((1,), (1,)), ((), ()))


def ocean_kernel(prof_ref, pts_ref, east_ref, north_ref, live_ref, vort_ref, diff_ref, out_ref, p_s, s_s):
    layers, points = prof_ref.shape
    slots = pts_ref.shape[0]
    per = LOW // layers
    for k in range(points // LOW):
        p_s[k * layers : (k + 1) * layers, :] = prof_ref[:, k * LOW : (k + 1) * LOW]
    lane = lax.broadcasted_iota(jnp.int32, (LOW, LOW), 1)
    block = lane // layers

    def pick(index, count, product):
        low = jnp.broadcast_to(index % LOW, (LOW, LOW))
        high = jnp.broadcast_to(index // LOW, (LOW, LOW)) - block
        hot = jnp.where(low == lane, 1.0, 0.0).astype(jnp.bfloat16)
        acc = jnp.zeros((LOW, LOW), jnp.float32)
        for m in range(-(-count // per)):
            acc = acc + jnp.where(high == m * per, product(hot, m), 0.0)
        return sum(acc[:, i * layers : (i + 1) * layers] for i in range(per))

    def from_points(hot, m):
        return lax.dot_general(hot, p_s[m * LOW : (m + 1) * LOW, :], NT, preferred_element_type=jnp.float32)

    s_s[...] = jnp.zeros_like(s_s)
    for j in range(slots // LOW):
        s = pick(pts_ref[j * LOW : (j + 1) * LOW, :], points // LOW, from_points)
        s_s[:, j * layers : (j + 1) * layers] = s.astype(jnp.bfloat16)

    def from_slots(hot, m):
        return jnp.dot(hot, s_s[:, m * LOW : (m + 1) * LOW], preferred_element_type=jnp.float32)

    for j in range(slots // LOW):
        rows = slice(j * LOW, (j + 1) * LOW)
        gap = pick(east_ref[rows, :], slots // LOW, from_slots) - pick(north_ref[rows, :], slots // LOW, from_slots)
        gap = gap.T
        s = s_s[:, j * layers : (j + 1) * layers].astype(jnp.float32).T
        upper = jnp.concatenate([s[:1], s[:-1]], axis=0)
        lower = jnp.concatenate([s[1:], jnp.zeros_like(s[:1])], axis=0)
        out_ref[:, rows] = live_ref[:, rows] * (
            vort_ref[:, rows] * gap + diff_ref[:, rows] * (upper - 2.0 * s + lower)
        )


def ocean(profile, pts, count, nbr, vort, diff):
    layers, points = profile.shape
    slots = pts.shape[0]
    per = LOW // layers
    lanes = -(-(slots // LOW) // per) * LOW
    live = (jnp.arange(slots, dtype=jnp.int32) < count).astype(jnp.float32)[None]
    return pl.pallas_call(
        ocean_kernel,
        out_shape=jax.ShapeDtypeStruct((layers, slots), jnp.float32),
        scratch_shapes=[
            pltpu.VMEM((points // LOW * layers, LOW), jnp.bfloat16),
            pltpu.VMEM((LOW, lanes), jnp.bfloat16),
        ],
        name="ocean",
    )(profile, pts[:, None], nbr[0][:, None], nbr[1][:, None], live, vort, diff)


def contract(weights, operand):
    return lax.dot_general(
        weights, operand, (((0,), (0,)), ((), ())), preferred_element_type=jnp.float32
    )


def on_device(
    spectrum,
    mask,
    courant,
    proj_a,
    proj_b,
    proj_c,
    proj_d,
    stokes_kernel,
    tile_points,
    tile_counts,
    tile_nbr,
    vorticity,
    diffusivity,
):
    comps, rows, lon = spectrum.shape
    margin = 2 * ADV
    bands, dests = lax.axis_size("lat"), lax.axis_size("comp")
    band_index = lax.axis_index("lat")
    sea = jnp.pad(mask.astype(jnp.float32), ((margin, margin), (0, 0)))
    mask_rows = lax.dynamic_slice_in_dim(sea, band_index * rows, rows + 2 * margin, 0)
    up = [(i, i + 1) for i in range(bands - 1)]
    down = [(j, i) for i, j in up]

    def edge(part):
        return lax.optimization_barrier(part).astype(jnp.bfloat16).transpose(1, 0, 2)

    halo_up = lax.ppermute(edge(spectrum[:, rows - margin :]), "lat", up)
    halo_dn = lax.ppermute(edge(spectrum[:, :margin]), "lat", down)
    weights = [lax.all_gather(w, "comp", axis=0, tiled=True) for w in (proj_a, proj_b, proj_c, proj_d)]
    band = advect(spectrum, halo_up, halo_dn, mask_rows, courant.T, dests)
    points = lax.all_to_all(band.astype(jnp.float16), "comp", split_axis=0, concat_axis=0)
    chunk = points.shape[2]
    points = points.reshape(dests * comps, chunk)
    own = points.astype(jnp.float32)
    points = own.astype(jnp.bfloat16)
    product = (contract(weights[0], points) * contract(weights[1], points)).astype(jnp.bfloat16)
    delta = time_step * (contract(weights[2], product) - own * contract(weights[3], product))
    profile = lax.dot_general(
        stokes_kernel, own + delta, (((0,), (0,)), ((), ())), precision=lax.Precision.HIGHEST
    ).astype(jnp.bfloat16)
    group = lax.all_gather(profile, "comp", axis=1, tiled=True)
    back = lax.all_to_all(
        delta.astype(jnp.bfloat16).reshape(dests, comps, chunk), "comp", split_axis=0, concat_axis=0
    )
    force = ocean(group, tile_points[0, 0], tile_counts[0, 0], tile_nbr[0, 0], vorticity[0, 0], diffusivity[0, 0])
    return finish(band, back, rows, lon), force[None, None]


def solution(mesh):
    return jax.shard_map(
        on_device,
        mesh=mesh,
        in_specs=(
            P("comp", "lat", None),
            P(),
            P(None, "comp"),
            P("comp", None),
            P("comp", None),
            P("comp", None),
            P("comp", None),
            P(),
            P("lat", "comp", None),
            P("lat", "comp"),
            P("lat", "comp", None, None),
            P("lat", "comp", None, None),
            P("lat", "comp", None, None),
        ),
        out_specs=(P("comp", "lat", None), P("lat", "comp", None, None)),
        check_vma=False,
    )
```

time: 324 us -> 284 us (0.88)
  Pallas kernels: 152 us -> 114 us
    pallas_call x2 -> x1, Pallas kernels: 43.4 us -> 10.6 us  [ocean(): pl.pallas_call(ocean_kernel, out_shape=jax.ShapeDtypeStruct((layers, slot...]
    pallas_call x1, Pallas kernels: 99.3 us -> 93.9 us  [advect(): pl.pallas_call(functools.partial(advect_kernel, rows, chunk), grid=(pl.cd...]
    unnamed x22 -> x23, local copies, waits for them, and re-layouts: 7.95 us -> 3.28 us
  transfers between devices with their start and end apart: 9 -> 9, of which waited for: 4 -> 4; matrix products, arithmetic and copies ran while one was open for 18% -> 19% of each run, Pallas kernels for 44% -> 37%
where the time goes in v2:
time: 284 us; the launch traced here: 282 us
  Pallas kernels  114 us (40%)
  waiting for transfers between devices  67.8 us (24%)
  matrix products  42.1 us (15%)
  local copies, waits for them, and re-layouts  19.8 us (7%)
  starting transfers between devices  15.4 us (5%)
  between operations  14.6 us (5%)
  other arithmetic  8.82 us (3%)
    pallas_call x1, Pallas kernels, advect(): pl.pallas_call(functools.partial(advect_kernel, rows, chunk), grid=(pl.cd...  93.9 us
    dot_general x4, matrix products, contract(): lax.dot_general(weights, operand, (((0,), (0,)), ((), ())), preferred_ele...  32.9 us
    all_to_all x1, waiting for transfers between devices, on_device(): lax.all_to_all(band.astype(jnp.float16), 'comp', split_axis=0, concat_axi...  30.9 us
    all_gather x1, waiting for transfers between devices, on_device(): group = lax.all_gather(profile, 'comp', axis=1, tiled=True)  21.2 us
    pallas_call x1, Pallas kernels, ocean(): pl.pallas_call(ocean_kernel, out_shape=jax.ShapeDtypeStruct((layers, slot...  10.6 us
    dot_general x1, matrix products, on_device(): lax.dot_general(stokes_kernel, own + delta, (((0,), (0,)), ((), ())), pre...  9.17 us
    ppermute x1, waiting for transfers between devices, on_device(): halo_up = lax.ppermute(edge(spectrum[:, rows - margin:]), 'lat', up)  9.12 us
    pallas_call x1, Pallas kernels, finish(): pl.pallas_call(functools.partial(finish_kernel, rows), grid=(pl.cdiv(comp...  9.06 us
  transfers between devices with their start and end apart: 9, of which 4 were waited for; matrix products, arithmetic and copies ran while one was open for 19% of the time, Pallas kernels for 37%

profile of v2, /device:TPU:3, one launch (start us, length us, event | category | flops | bytes accessed | tf_op | source)
XLA Modules:
  0.0 282.0 jit_solution(16190947161999258364)
XLA Ops:
  7.2 0.0 copy-start
  7.2 0.0 all-gather.6.cloned.1.call-start
  7.2 0.7 all-gather.6.cloned.1.call-update
  7.9 0.0 all-gather.8.cloned.1.call-start
  8.0 0.7 all-gather.8.cloned.1.call-update
  8.7 0.0 all-gather.10.cloned.1.call-start
  8.7 0.7 all-gather.10.cloned.1.call-update
  9.4 3.0 %fusion.12 = (bf16[144,4,512]{2,1,0:T(4,128)(2,1)S(1)}, bf16[144,4,512]{2,1,0:T(4,128)(2,1)S(1)}) fusion(f32[144,16,512]{2,1,0:T(8,128)} %param.13), kind=kLoop, calls=%fused_computation.17 | loop fusion | bytes 2359296 | tf_op jit(solution)/shard_map/slice | solution.py:253
  12.4 0.1 copy.30
  12.5 3.2 %collective-permute-start = (bf16[4,144,512]{2,1,0:T(8,128)(2,1)S(1)}, bf16[4,144,512]{2,1,0:T(8,128)(2,1)S(1)}, u32[]{:S(2)}, u32[]{:S(2)}) collective-permute-start(bf16[4,144,512]{2,1,0:T(8,128)(2,1)S(1)} %bitcast.47), channel_id=1, source_target_pairs={{0,8},{8,16},{16,24},{1,9},{9,17},{17,25},{2,10},{10,18},{18,26},{... | collective-permute-start | bytes 1769480 | tf_op jit(solution)/shard_map/ppermute | solution.py:252
  15.7 0.1 copy.31
  15.9 1.3 collective-permute-start.1
  17.2 0.7 copy.23
  18.0 0.6 pad_dynamic-slice_fusion.mask_ref
  18.6 9.1 %collective-permute-done.up_ref = bf16[4,144,512]{2,1,0:T(8,128)(2,1)S(1)} collective-permute-done((bf16[4,144,512]{2,1,0:T(8,128)(2,1)S(1)}, bf16[4,144,512]{2,1,0:T(8,128)(2,1)S(1)}, u32[]{:S(2)}, u32[]{:S(2)}) %collective-permute-start) | collective-permute-done | bytes 589856 | tf_op jit(solution)/shard_map/ppermute | solution.py:252
  27.7 4.0 %collective-permute-done.1.dn_ref = bf16[4,144,512]{2,1,0:T(8,128)(2,1)S(1)} collective-permute-done((bf16[4,144,512]{2,1,0:T(8,128)(2,1)S(1)}, bf16[4,144,512]{2,1,0:T(8,128)(2,1)S(1)}, u32[]{:S(2)}, u32[]{:S(2)}) %collective-permute-start.1) | collective-permute-done | bytes 589856 | tf_op jit(solution)/shard_map/ppermute | solution.py:253
  31.7 0.0 copy-done.4
  31.7 0.8 copy-done.5
  32.5 93.9 %advect.1.band_ref = f32[8,144,1024]{2,1,0:T(8,128)} custom-call(f32[2304,512]{1,0:T(8,128)} %bitcast.45, bf16[4,144,512]{2,1,0:T(8,128)(2,1)} %copy-done.4, bf16[4,144,512]{2,1,0:T(8,128)(2,1)} %copy-done.5, f32[24,512]{1,0:T(8,128)} %pad_dynamic-slice_fusion.mask_ref, f32[144,2]{1,0:T(8,128)} %bitcast.52), custom_call_target="tpu_custom_call" | custom-call | tf_op jit(solution)/shard_map/advect/pallas_call | solution.py:104
  126.4 4.2 %convert_element_type.49 = f16[8,144,1024]{2,1,0:T(8,128)(2,1)} convert(f32[8,144,1024]{2,1,0:T(8,128)} %advect.1.band_ref) | non-fusion elementwise | flops 1179648 | bytes 7077888 | tf_op jit(solution)/shard_map/convert_element_type | solution.py:256
  130.6 5.7 %all-to-all-start = ((f16[8,144,1024]{2,1,0:T(8,128)(2,1)}), f16[8,144,1024]{2,1,0:T(8,128)(2,1)S(1)}, u32[]{:S(2)}, u32[]{:S(2)}) async-start(f16[8,144,1024]{2,1,0:T(8,128)(2,1)} %convert_element_type.49), calls=%async_computation | async-start | bytes 4718592 | tf_op jit(solution)/shard_map/all_to_all | solution.py:256
  136.3 0.0 all-gather.12.cloned.1.call-start
  136.3 0.6 all-gather.12.cloned.1.call-update
  136.9 30.9 %all-to-all-done = f16[8,144,1024]{2,1,0:T(8,128)(2,1)S(1)} async-done(((f16[8,144,1024]{2,1,0:T(8,128)(2,1)}), f16[8,144,1024]{2,1,0:T(8,128)(2,1)S(1)}, u32[]{:S(2)}, u32[]{:S(2)}) %all-to-all-start) | async-done | bytes 2359328 | tf_op jit(solution)/shard_map/all_to_all | solution.py:256
  167.7 4.0 %fusion.5 = (bf16[1152,1024]{1,0:T(8,128)(2,1)}, f32[1152,1024]{1,0:T(8,128)}) fusion(f16[8,144,1024]{2,1,0:T(8,128)(2,1)S(1)} %all-to-all-done), kind=kLoop, calls=%fused_computation.8 | loop fusion | flops 2359296 | bytes 9437184 | tf_op jit(solution)/shard_map/convert_element_type | solution.py:260
  171.7 6.3 %copy.24 = f32[1152,1024]{0,1:T(8,128)} copy(f32[1152,1024]{1,0:T(8,128)} %get-tuple-element.5) | data formatting | bytes 9437184 | tf_op jit(solution)/shard_map/convert_element_type | solution.py:259
  178.0 7.0 %fusion.14 = f32[1024,1152]{1,0:T(8,128)} fusion(bf16[1152,1024]{1,0:T(8,128)(2,1)S(1)} %copy-done.3, bf16[1152,1152]{1,0:T(8,128)(2,1)} %all-gather.6.cloned.1.call-done), kind=kOutput, calls=%fused_computation.19 | convolution fusion | flops 2717908992 | bytes 9732096 | tf_op jit(solution)/shard_map/dot_general | solution.py:220
  185.0 7.4 %fusion.4 = bf16[1024,1152]{1,0:T(8,128)(2,1)S(1)} fusion(f32[1024,1152]{1,0:T(8,128)} %fusion.14, bf16[1152,1024]{1,0:T(8,128)(2,1)} %get-tuple-element.4, bf16[1152,1152]{1,0:T(8,128)(2,1)} %all-gather.8.cloned.1.call-done), kind=kOutput, calls=%fused_computation.6 | convolution fusion | flops 2720268288 | bytes 12091392 | tf_op jit(solution)/shard_map/dot_general | solution.py:220
  192.4 0.0 all-gather.10.cloned.1.call-done
  192.4 7.7 %fusion.15 = f32[1024,1152]{1,0:T(8,128)} fusion(bf16[1024,1152]{1,0:T(8,128)(2,1)S(1)} %fusion.4, bf16[1152,1152]{1,0:T(8,128)(2,1)} %all-gather.10.cloned.1.call-done), kind=kOutput, calls=%fused_computation.20 | convolution fusion | flops 2717908992 | bytes 9732096 | tf_op jit(solution)/shard_map/dot_general | solution.py:220
  200.1 0.0 copy-done.2
  200.1 10.9 %fusion.13 = (bf16[1152,1024]{0,1:T(8,128)(2,1)S(1)}, f32[1152,1024]{0,1:T(8,128)}) fusion(f32[1152,1024]{0,1:T(8,128)} %copy.24, bf16[1024,1152]{1,0:T(8,128)(2,1)} %copy-done.2, bf16[1152,1152]{1,0:T(8,128)(2,1)} %all-gather.12.cloned.1.call-done, f32[1024,1152]{1,0:T(8,128)} %fusion.15), kind=kOutput, calls=%fused_computation.18 | convolution fusion | flops 2722627584 | bytes 21528576 | tf_op jit(solution)/shard_map/dot_general | solution.py:220
  211.0 2.5 copy.25
  213.5 5.1 %all-to-all-start.1 = ((bf16[8,144,1024]{2,1,0:T(8,128)(2,1)}), bf16[8,144,1024]{2,1,0:T(8,128)(2,1)S(1)}, u32[]{:S(2)}, u32[]{:S(2)}) async-start(bf16[8,144,1024]{2,1,0:T(8,128)(2,1)} %bitcast.44), calls=%async_computation.1 | async-start | bytes 4718592 | tf_op jit(solution)/shard_map/all_to_all | solution.py:267
  218.5 0.0 all-gather.14.cloned.1.call-start
  218.6 0.0 copy-start.7
  218.6 0.0 copy-start.8
  218.6 9.2 %fusion.9 = bf16[64,1024]{1,0:T(8,128)(2,1)} fusion(f32[1152,64]{0,1:T(8,128)S(1)} %copy-done, f32[1152,1024]{0,1:T(8,128)} %copy.24, f32[1152,1024]{0,1:T(8,128)} %get-tuple-element.9), kind=kOutput, calls=%fused_computation.10 | convolution fusion | flops 907214848 | bytes 9863168 | tf_op jit(solution)/shard_map/dot_general | solution.py:263
  227.8 0.0 all-gather.14.cloned.1.call-update
  227.8 1.4 copy.28.east_ref
  229.2 1.4 copy.29.north_ref
  230.6 1.3 copy.27.pts_ref
  232.6 0.6 compare_convert_fusion.live_ref
  233.2 21.2 %all-gather.14.cloned.1.call-done.prof_ref = bf16[64,8192]{1,0:T(8,128)(2,1)} async-done(((bf16[64,1024]{1,0:T(8,128)(2,1)}), bf16[64,8192]{1,0:T(8,128)(2,1)}) %all-gather.14.cloned.1.call-update) | async-done | bytes 1048592 | tf_op jit(solution)/shard_map/all_gather | solution.py:266
  254.3 10.6 %ocean.1 = f32[64,2048]{1,0:T(8,128)} custom-call(bf16[64,8192]{1,0:T(8,128)(2,1)} %all-gather.14.cloned.1.call-done.prof_ref, s32[2048,1]{1,0:T(8,128)} %copy.27.pts_ref, s32[2048,1]{1,0:T(8,128)} %copy.28.east_ref, s32[2048,1]{1,0:T(8,128)} %copy.29.north_ref, f32[1,2048]{1,0:T(1,128)} %compare_convert_fusion.live_ref, f32[64,2048]{1,0:T(8,128)} %bitcast.49, ...), custom_call_target="tpu_custom_call" | custom-call | tf_op jit(solution)/shard_map/ocean/pallas_call | solution.py:208
  265.0 0.0 all-to-all-done.1.delta_ref
  265.0 1.5 copy-done.1
  266.4 9.1 %finish.1 = f32[2304,512]{1,0:T(8,128)} custom-call(f32[8,144,1024]{2,1,0:T(8,128)} %advect.1.band_ref, bf16[8,144,1024]{2,1,0:T(8,128)(2,1)} %copy-done.1), custom_call_target="tpu_custom_call" | custom-call | tf_op jit(solution)/shard_map/finish/pallas_call | solution.py:146
  (18 shorter events, 0.1 us)
Async XLA Ops:
  7.2 211.4 %copy-start = (f32[1152,64]{0,1:T(8,128)S(1)}, f32[1152,64]{0,1:T(8,128)}, u32[]{:S(2)}) copy-start(f32[1152,64]{0,1:T(8,128)} %param.20) | copy-start | bytes 884740
  7.2 170.8 %all-gather.6.cloned.1.call-start = ((), (), s32[]{:S(2)}) async-start(), calls=%async_computation.2 | async-start | bytes 2985984 | tf_op jit(solution)/shard_map/all_gather | solution.py:254
  7.9 9.3 %copy-start.6 = (s32[64,512]{1,0:T(8,128)S(1)}, s32[64,512]{1,0:T(8,128)}, u32[]{:S(2)}) copy-start(s32[64,512]{1,0:T(8,128)} %param.14) | copy-start | bytes 393220
  7.9 177.1 %all-gather.8.cloned.1.call-start = ((), (), s32[]{:S(2)}) async-start(), calls=%async_computation.3 | async-start | bytes 2985984 | tf_op jit(solution)/shard_map/all_gather | solution.py:254
  8.7 8.5 %copy-start.9 = (f32[2,144]{1,0:T(2,128)S(1)}, f32[2,144]{1,0:T(2,128)}, u32[]{:S(2)}) copy-start(f32[2,144]{1,0:T(2,128)} %param.15) | copy-start | bytes 3460
  8.7 183.7 %all-gather.10.cloned.1.call-start = ((), (), s32[]{:S(2)}) async-start(), calls=%async_computation.4 | async-start | bytes 2985984 | tf_op jit(solution)/shard_map/all_gather | solution.py:254
  12.5 15.2 %collective-permute-start = (bf16[4,144,512]{2,1,0:T(8,128)(2,1)S(1)}, bf16[4,144,512]{2,1,0:T(8,128)(2,1)S(1)}, u32[]{:S(2)}, u32[]{:S(2)}) collective-permute-start(bf16[4,144,512]{2,1,0:T(8,128)(2,1)S(1)} %bitcast.47), channel_id=1, source_target_pairs={{0,8},{8,16},{16,24},{1,9},{9,17},{17,25},{2,10},{10,18},{18,26},{... | collective-permute-start | bytes 1769480 | tf_op jit(solution)/shard_map/ppermute | solution.py:252
  15.9 15.8 %collective-permute-start.1 = (bf16[4,144,512]{2,1,0:T(8,128)(2,1)S(1)}, bf16[4,144,512]{2,1,0:T(8,128)(2,1)S(1)}, u32[]{:S(2)}, u32[]{:S(2)}) collective-permute-start(bf16[4,144,512]{2,1,0:T(8,128)(2,1)S(1)} %bitcast.48), channel_id=1, source_target_pairs={{8,0},{16,8},{24,16},{9,1},{17,9},{25,17},{10,2},{18,10},{26,18},{... | collective-permute-start | bytes 1769480 | tf_op jit(solution)/shard_map/ppermute | solution.py:253
  27.7 4.0 %copy-start.4 = (bf16[4,144,512]{2,1,0:T(8,128)(2,1)}, bf16[4,144,512]{2,1,0:T(8,128)(2,1)S(1)}, u32[]{:S(2)}) copy-start(bf16[4,144,512]{2,1,0:T(8,128)(2,1)S(1)} %collective-permute-done.up_ref) | copy-start | bytes 1769476
  31.7 0.8 copy-start.5
  130.6 37.1 %all-to-all-start = ((f16[8,144,1024]{2,1,0:T(8,128)(2,1)}), f16[8,144,1024]{2,1,0:T(8,128)(2,1)S(1)}, u32[]{:S(2)}, u32[]{:S(2)}) async-start(f16[8,144,1024]{2,1,0:T(8,128)(2,1)} %convert_element_type.49), calls=%async_computation | async-start | bytes 4718592 | tf_op jit(solution)/shard_map/all_to_all | solution.py:256
  136.3 63.8 %all-gather.12.cloned.1.call-start = ((), (), s32[]{:S(2)}) async-start(), calls=%async_computation.5 | async-start | bytes 2985984 | tf_op jit(solution)/shard_map/all_gather | solution.py:254
  171.7 6.3 %copy-start.3 = (bf16[1152,1024]{1,0:T(8,128)(2,1)S(1)}, bf16[1152,1024]{1,0:T(8,128)(2,1)}, u32[]{:S(2)}) copy-start(bf16[1152,1024]{1,0:T(8,128)(2,1)} %get-tuple-element.4) | copy-start | bytes 7077892
  192.4 7.7 %copy-start.2 = (bf16[1024,1152]{1,0:T(8,128)(2,1)}, bf16[1024,1152]{1,0:T(8,128)(2,1)S(1)}, u32[]{:S(2)}) copy-start(bf16[1024,1152]{1,0:T(8,128)(2,1)S(1)} %fusion.4) | copy-start | bytes 7077892
  213.5 51.5 %all-to-all-start.1 = ((bf16[8,144,1024]{2,1,0:T(8,128)(2,1)}), bf16[8,144,1024]{2,1,0:T(8,128)(2,1)S(1)}, u32[]{:S(2)}, u32[]{:S(2)}) async-start(bf16[8,144,1024]{2,1,0:T(8,128)(2,1)} %bitcast.44), calls=%async_computation.1 | async-start | bytes 4718592 | tf_op jit(solution)/shard_map/all_to_all | solution.py:267
  218.5 35.8 %all-gather.14.cloned.1.call-start = ((), (), s32[]{:S(2)}) async-start(), calls=%async_computation.6 | async-start | bytes 1179648 | tf_op jit(solution)/shard_map/all_gather | solution.py:266
  218.6 9.2 %copy-start.7 = (s32[1,1,2,2048]{3,2,1,0:T(2,128)S(1)}, s32[1,1,2,2048]{3,2,1,0:T(2,128)}, u32[]{:S(2)}) copy-start(s32[1,1,2,2048]{3,2,1,0:T(2,128)} %param.23) | copy-start | bytes 49156
  218.6 12.0 %copy-start.8 = (s32[1,1,2048]{2,1,0:T(1,128)S(1)}, s32[1,1,2048]{2,1,0:T(1,128)}, u32[]{:S(2)}) copy-start(s32[1,1,2048]{2,1,0:T(1,128)} %param.21) | copy-start | bytes 24580
  265.0 1.5 copy-start.1
Sparse Core Ops, SparseCore 0:
  9.9 31.7 all-gather.5
  43.5 30.5 all-gather.7
  76.0 30.3 all-gather.9
  138.7 40.3 all-gather.11
  227.9 26.3 all-gather.13

commit v3 on v2

--- a/solution.py
+++ b/solution.py
@@ -12,6 +12,7 @@
 CB = 16
 LANES = 128
 LOW = 256
+PIECES = 2
 
 
 def half_limited(b, f):
@@ -95,30 +96,34 @@
                 before = flux
 
 
-def advect(spectrum, halo_up, halo_dn, mask_rows, cour, dests):
+def advect(spectrum, halo_up, halo_dn, mask_rows, cour, dests, first, size):
     comps, rows, lon = spectrum.shape
     chunk = rows * lon // dests
     margin = 2 * ADV
+    skip = first // CB
     total = rows + 2 * margin
     blk = pl.BlockSpec((dests, CB, chunk), lambda i: (0, i, 0))
     return pl.pallas_call(
         functools.partial(advect_kernel, rows, chunk),
-        grid=(pl.cdiv(comps, CB),),
+        grid=(pl.cdiv(size, CB),),
         in_specs=[
-            pl.BlockSpec((CB * rows, lon), lambda i: (i, 0)),
-            pl.BlockSpec((margin, CB, lon), lambda i: (0, i, 0)),
-            pl.BlockSpec((margin, CB, lon), lambda i: (0, i, 0)),
+            pl.BlockSpec((CB * rows, lon), lambda i: (i + skip, 0)),
+            pl.BlockSpec((margin, CB, lon), lambda i: (0, i + skip, 0)),
+            pl.BlockSpec((margin, CB, lon), lambda i: (0, i + skip, 0)),
             pl.BlockSpec((total, lon), lambda i: (0, 0)),
-            pl.BlockSpec((CB, 2), lambda i: (i, 0)),
+            pl.BlockSpec((CB, 2), lambda i: (i + skip, 0)),
         ],
         out_specs=blk,
-        out_shape=jax.ShapeDtypeStruct((dests, comps, chunk), jnp.float32),
+        out_shape=jax.ShapeDtypeStruct((dests, size, chunk), jnp.float32),
         scratch_shapes=[
             pltpu.VMEM((total, 8, lon), jnp.float32),
             pltpu.VMEM((total, 8, lon), jnp.float32),
             pltpu.VMEM((2 * margin, CB, lon), jnp.float32),
             pltpu.VMEM((lon // LANES, CB * rows, LANES), jnp.float32),
         ],
+        cost_estimate=pl.CostEstimate(
+            flops=size * rows * lon * 400, bytes_accessed=size * rows * lon * 8, transcendentals=0
+        ),
         name="advect",
     )(spectrum.reshape(comps * rows, lon), halo_up, halo_dn, mask_rows, cour)
 
@@ -252,8 +257,16 @@
     halo_up = lax.ppermute(edge(spectrum[:, rows - margin :]), "lat", up)
     halo_dn = lax.ppermute(edge(spectrum[:, :margin]), "lat", down)
     weights = [lax.all_gather(w, "comp", axis=0, tiled=True) for w in (proj_a, proj_b, proj_c, proj_d)]
-    band = advect(spectrum, halo_up, halo_dn, mask_rows, courant.T, dests)
-    points = lax.all_to_all(band.astype(jnp.float16), "comp", split_axis=0, concat_axis=0)
+    bands_of, points_of = [], []
+    width = pl.cdiv(pl.cdiv(comps, CB), PIECES) * CB
+    for first in range(0, comps, width):
+        piece = advect(
+            spectrum, halo_up, halo_dn, mask_rows, courant.T, dests, first, min(width, comps - first)
+        )
+        bands_of.append(piece)
+        points_of.append(lax.all_to_all(piece.astype(jnp.float16), "comp", split_axis=0, concat_axis=0))
+    band = jnp.concatenate(bands_of, axis=1)
+    points = jnp.concatenate(points_of, axis=1)
     chunk = points.shape[2]
     points = points.reshape(dests * comps, chunk)
     own = points.astype(jnp.float32)

time: 284 us -> 276 us (0.972)
  waiting for transfers between devices: 67.8 us -> 32.6 us
  blocking collectives: 0 us -> 20.5 us
  other arithmetic: 8.82 us -> 13.6 us
    all_to_all x1, waiting for transfers between devices: 30.9 us -> 0.01 us  [on_device(): lax.all_to_all(piece.astype(jnp.float16), 'comp', split_axis=0, concat_ax...]
    all_to_all x0 -> x1, blocking collectives: none -> 20.5 us  [on_device(): lax.all_to_all(piece.astype(jnp.float16), 'comp', split_axis=0, concat_ax...]
    concatenate x0 -> x2, other arithmetic: none -> 5.06 us  [the longest x1 4.36 us: on_device(): band = jnp.concatenate(bands_of, axis=1)]
    all_gather x1, waiting for transfers between devices: 21.2 us -> 16.8 us  [on_device(): group = lax.all_gather(profile, 'comp', axis=1, tiled=True)]
    pallas_call x1 -> x2, Pallas kernels: 93.9 us -> 95.7 us  [advect(): pl.pallas_call(functools.partial(advect_kernel, rows, chunk), grid=(pl.cd...]
  transfers between devices with their start and end apart: 9 -> 9, of which waited for: 4 -> 3; matrix products, arithmetic and copies ran while one was open for 19% -> 22% of each run, Pallas kernels for 37% -> 39%
where the time goes in v3:
time: 276 us; the launch traced here: 274 us
  Pallas kernels  115 us (42%)
  matrix products  42.1 us (15%)
  waiting for transfers between devices  32.6 us (12%)
  blocking collectives  20.5 us (7%)
  local copies, waits for them, and re-layouts  19 us (7%)
  starting transfers between devices  16.3 us (6%)
  between operations  14.6 us (5%)
  other arithmetic  13.6 us (5%)
    pallas_call x2, Pallas kernels, advect(): pl.pallas_call(functools.partial(advect_kernel, rows, chunk), grid=(pl.cd...  95.7 us
    dot_general x4, matrix products, contract(): lax.dot_general(weights, operand, (((0,), (0,)), ((), ())), preferred_ele...  32.9 us
    all_to_all x1, blocking collectives, on_device(): lax.all_to_all(piece.astype(jnp.float16), 'comp', split_axis=0, concat_ax...  20.5 us
    all_gather x1, waiting for transfers between devices, on_device(): group = lax.all_gather(profile, 'comp', axis=1, tiled=True)  16.8 us
    pallas_call x1, Pallas kernels, ocean(): pl.pallas_call(ocean_kernel, out_shape=jax.ShapeDtypeStruct((layers, slot...  10.6 us
    dot_general x1, matrix products, on_device(): lax.dot_general(stokes_kernel, own + delta, (((0,), (0,)), ((), ())), pre...  9.18 us
    ppermute x1, waiting for transfers between devices, on_device(): halo_up = lax.ppermute(edge(spectrum[:, rows - margin:]), 'lat', up)  9.12 us
    pallas_call x1, Pallas kernels, finish(): pl.pallas_call(functools.partial(finish_kernel, rows), grid=(pl.cdiv(comp...  9.07 us
  transfers between devices with their start and end apart: 9, of which 3 were waited for; matrix products, arithmetic and copies ran while one was open for 22% of the time, Pallas kernels for 39%

profile of v3, /device:TPU:3, one launch (start us, length us, event | category | flops | bytes accessed | tf_op | source)
XLA Modules:
  0.0 274.0 jit_solution(6493854767570638180)
XLA Ops:
  7.2 0.0 copy-start
  7.2 0.0 all-gather.6.cloned.1.call-start
  7.2 0.7 all-gather.6.cloned.1.call-update
  7.9 0.0 all-gather.8.cloned.1.call-start
  8.0 0.7 all-gather.8.cloned.1.call-update
  8.7 0.0 all-gather.10.cloned.1.call-start
  8.7 0.7 all-gather.10.cloned.1.call-update
  9.4 3.0 %fusion.12 = (bf16[144,4,512]{2,1,0:T(4,128)(2,1)S(1)}, bf16[144,4,512]{2,1,0:T(4,128)(2,1)S(1)}) fusion(f32[144,16,512]{2,1,0:T(8,128)} %param.13), kind=kLoop, calls=%fused_computation.19 | loop fusion | bytes 2359296 | tf_op jit(solution)/shard_map/slice | solution.py:258
  12.4 0.1 copy.30
  12.5 3.2 %collective-permute-start = (bf16[4,144,512]{2,1,0:T(8,128)(2,1)S(1)}, bf16[4,144,512]{2,1,0:T(8,128)(2,1)S(1)}, u32[]{:S(2)}, u32[]{:S(2)}) collective-permute-start(bf16[4,144,512]{2,1,0:T(8,128)(2,1)S(1)} %bitcast.50), channel_id=1, source_target_pairs={{0,8},{8,16},{16,24},{1,9},{9,17},{17,25},{2,10},{10,18},{18,26},{... | collective-permute-start | bytes 1769480 | tf_op jit(solution)/shard_map/ppermute | solution.py:257
  15.7 0.1 copy.31
  15.9 1.3 collective-permute-start.1
  17.2 0.7 copy.23
  18.0 0.6 pad_dynamic-slice_fusion.mask_ref
  18.6 9.1 %collective-permute-done.up_ref = bf16[4,144,512]{2,1,0:T(8,128)(2,1)S(1)} collective-permute-done((bf16[4,144,512]{2,1,0:T(8,128)(2,1)S(1)}, bf16[4,144,512]{2,1,0:T(8,128)(2,1)S(1)}, u32[]{:S(2)}, u32[]{:S(2)}) %collective-permute-start) | collective-permute-done | bytes 589856 | tf_op jit(solution)/shard_map/ppermute | solution.py:257
  27.7 4.0 %collective-permute-done.1.dn_ref = bf16[4,144,512]{2,1,0:T(8,128)(2,1)S(1)} collective-permute-done((bf16[4,144,512]{2,1,0:T(8,128)(2,1)S(1)}, bf16[4,144,512]{2,1,0:T(8,128)(2,1)S(1)}, u32[]{:S(2)}, u32[]{:S(2)}) %collective-permute-start.1) | collective-permute-done | bytes 589856 | tf_op jit(solution)/shard_map/ppermute | solution.py:258
  31.7 0.8 copy-done.4
  32.5 42.8 %advect.3 = f32[8,64,1024]{2,1,0:T(8,128)} custom-call(f32[2304,512]{1,0:T(8,128)} %bitcast.44, bf16[4,144,512]{2,1,0:T(8,128)(2,1)} %copy-done.3, bf16[4,144,512]{2,1,0:T(8,128)(2,1)} %copy-done.4, f32[24,512]{1,0:T(8,128)} %pad_dynamic-slice_fusion.mask_ref, f32[144,2]{1,0:T(8,128)} %bitcast.48), custom_call_target="tpu_custom_call" | custom-call | flops 209715200 | bytes 4194304 | tf_op jit(solution)/shard_map/advect/pallas_call | solution.py:106
  75.3 2.7 %convert_element_type.53 = f16[8,64,1024]{2,1,0:T(8,128)(2,1)} convert(f32[8,64,1024]{2,1,0:T(8,128)} %advect.3) | non-fusion elementwise | flops 524288 | bytes 3145728 | tf_op jit(solution)/shard_map/convert_element_type | solution.py:267
  78.0 5.7 %all-to-all-start.1 = ((f16[8,64,1024]{2,1,0:T(8,128)(2,1)}), f16[8,64,1024]{2,1,0:T(8,128)(2,1)S(1)}, u32[]{:S(2)}, u32[]{:S(2)}) async-start(f16[8,64,1024]{2,1,0:T(8,128)(2,1)} %convert_element_type.53), calls=%async_computation.1 | async-start | bytes 2097152 | tf_op jit(solution)/shard_map/all_to_all | solution.py:267
  83.7 0.6 all-gather.12.cloned.1.call-update
  84.3 53.0 %advect.2 = f32[8,80,1024]{2,1,0:T(8,128)} custom-call(f32[2304,512]{1,0:T(8,128)} %bitcast.45, bf16[4,144,512]{2,1,0:T(8,128)(2,1)} %copy-done.3, bf16[4,144,512]{2,1,0:T(8,128)(2,1)} %copy-done.4, f32[24,512]{1,0:T(8,128)} %pad_dynamic-slice_fusion.mask_ref, f32[144,2]{1,0:T(8,128)} %bitcast.49), custom_call_target="tpu_custom_call" | custom-call | flops 262144000 | bytes 5242880 | tf_op jit(solution)/shard_map/advect/pallas_call | solution.py:106
  137.2 2.0 convert_element_type.52
  139.2 0.0 all-to-all-done.1
  139.2 20.5 %all_to_all.15 = f16[8,80,1024]{2,1,0:T(8,128)(2,1)S(1)} all-to-all(f16[8,80,1024]{2,1,0:T(8,128)(2,1)S(1)} %convert_element_type.52), channel_id=1, replica_groups=mesh['lat'=4,'comp'=8] {'comp'}, dimensions={0} | all-to-all | bytes 2621440 | tf_op jit(solution)/shard_map/all_to_all | solution.py:267
  159.7 0.7 pad_maximum_fusion.1
  160.4 3.2 %fusion.5 = (bf16[1152,1024]{1,0:T(8,128)(2,1)S(1)}, f32[1152,1024]{1,0:T(8,128)}) fusion(f16[8,144,1024]{2,1,0:T(8,128)(2,1)S(1)} %pad_maximum_fusion.1), kind=kLoop, calls=%fused_computation.10 | loop fusion | flops 2359296 | bytes 9437184 | tf_op jit(solution)/shard_map/convert_element_type | solution.py:273
  163.6 6.9 %copy.24 = f32[1152,1024]{0,1:T(8,128)} copy(f32[1152,1024]{1,0:T(8,128)} %get-tuple-element.5) | data formatting | bytes 9437184 | tf_op jit(solution)/shard_map/convert_element_type | solution.py:272
  170.5 7.0 %fusion.14 = f32[1024,1152]{1,0:T(8,128)} fusion(bf16[1152,1024]{1,0:T(8,128)(2,1)S(1)} %get-tuple-element.4, bf16[1152,1152]{1,0:T(8,128)(2,1)} %all-gather.6.cloned.1.call-done), kind=kOutput, calls=%fused_computation.21 | convolution fusion | flops 2717908992 | bytes 9732096 | tf_op jit(solution)/shard_map/dot_general | solution.py:225
  177.5 7.4 %fusion.4 = bf16[1024,1152]{1,0:T(8,128)(2,1)S(1)} fusion(f32[1024,1152]{1,0:T(8,128)} %fusion.14, bf16[1152,1024]{1,0:T(8,128)(2,1)} %copy-done.5, bf16[1152,1152]{1,0:T(8,128)(2,1)} %all-gather.8.cloned.1.call-done), kind=kOutput, calls=%fused_computation.7 | convolution fusion | flops 2720268288 | bytes 12091392 | tf_op jit(solution)/shard_map/dot_general | solution.py:225
  184.9 0.0 all-gather.10.cloned.1.call-done
  184.9 7.7 %fusion.15 = f32[1024,1152]{1,0:T(8,128)} fusion(bf16[1024,1152]{1,0:T(8,128)(2,1)S(1)} %fusion.4, bf16[1152,1152]{1,0:T(8,128)(2,1)} %all-gather.10.cloned.1.call-done), kind=kOutput, calls=%fused_computation.22 | convolution fusion | flops 2717908992 | bytes 9732096 | tf_op jit(solution)/shard_map/dot_general | solution.py:225
  192.6 10.9 %fusion.13 = (bf16[1152,1024]{0,1:T(8,128)(2,1)S(1)}, f32[1152,1024]{0,1:T(8,128)}) fusion(f32[1152,1024]{0,1:T(8,128)} %copy.24, bf16[1024,1152]{1,0:T(8,128)(2,1)} %copy-done.2, bf16[1152,1152]{1,0:T(8,128)(2,1)} %all-gather.12.cloned.1.call-done, f32[1024,1152]{1,0:T(8,128)} %fusion.15), kind=kOutput, calls=%fused_computation.20 | convolution fusion | flops 2722627584 | bytes 21528576 | tf_op jit(solution)/shard_map/dot_general | solution.py:225
  203.5 2.5 copy.25
  206.0 5.9 %all-to-all-start.2 = ((bf16[8,144,1024]{2,1,0:T(8,128)(2,1)}), bf16[8,144,1024]{2,1,0:T(8,128)(2,1)}, u32[]{:S(2)}, u32[]{:S(2)}) async-start(bf16[8,144,1024]{2,1,0:T(8,128)(2,1)} %bitcast.46), calls=%async_computation.2 | async-start | bytes 4718592 | tf_op jit(solution)/shard_map/all_to_all | solution.py:280
  212.0 0.0 copy-start.7
  212.0 0.0 copy-start.8
  212.0 9.2 %fusion.9 = bf16[64,1024]{1,0:T(8,128)(2,1)} fusion(f32[1152,64]{0,1:T(8,128)S(1)} %copy-done, f32[1152,1024]{0,1:T(8,128)} %copy.24, f32[1152,1024]{0,1:T(8,128)} %get-tuple-element.9), kind=kOutput, calls=%fused_computation.12 | convolution fusion | flops 907214848 | bytes 9863168 | tf_op jit(solution)/shard_map/dot_general | solution.py:276
  221.2 0.0 all-gather.14.cloned.1.call-update
  221.2 1.4 copy.28.east_ref
  222.6 1.4 copy.29.north_ref
  224.0 1.3 copy.27.pts_ref
  226.0 0.6 compare_convert_fusion.live_ref
  226.6 4.4 %pad_maximum_fusion.band_ref = f32[8,144,1024]{2,1,0:T(8,128)} fusion(f32[8,64,1024]{2,1,0:T(8,128)} %advect.3, f32[8,80,1024]{2,1,0:T(8,128)S(1)} %copy-done.1), kind=kLoop, calls=%fused_computation.1 | loop fusion | flops 1179648 | bytes 9437184 | tf_op jit(solution)/shard_map/concatenate | solution.py:268
  230.9 16.8 %all-gather.14.cloned.1.call-done.prof_ref = bf16[64,8192]{1,0:T(8,128)(2,1)} async-done(((bf16[64,1024]{1,0:T(8,128)(2,1)}), bf16[64,8192]{1,0:T(8,128)(2,1)}) %all-gather.14.cloned.1.call-update) | async-done | bytes 1048592 | tf_op jit(solution)/shard_map/all_gather | solution.py:279
  247.7 10.6 %ocean.1 = f32[64,2048]{1,0:T(8,128)} custom-call(bf16[64,8192]{1,0:T(8,128)(2,1)} %all-gather.14.cloned.1.call-done.prof_ref, s32[2048,1]{1,0:T(8,128)} %copy.27.pts_ref, s32[2048,1]{1,0:T(8,128)} %copy.28.east_ref, s32[2048,1]{1,0:T(8,128)} %copy.29.north_ref, f32[1,2048]{1,0:T(1,128)} %compare_convert_fusion.live_ref, f32[64,2048]{1,0:T(8,128)} %bitcast.52, ...), custom_call_target="tpu_custom_call" | custom-call | tf_op jit(solution)/shard_map/ocean/pallas_call | solution.py:213
  258.4 0.0 all-to-all-done.2.delta_ref
  258.4 9.1 %finish.1 = f32[2304,512]{1,0:T(8,128)} custom-call(f32[8,144,1024]{2,1,0:T(8,128)} %pad_maximum_fusion.band_ref, bf16[8,144,1024]{2,1,0:T(8,128)(2,1)} %all-to-all-done.2.delta_ref), custom_call_target="tpu_custom_call" | custom-call | tf_op jit(solution)/shard_map/finish/pallas_call | solution.py:151
  (23 shorter events, 0.1 us)
Async XLA Ops:
  7.2 204.8 %copy-start = (f32[1152,64]{0,1:T(8,128)S(1)}, f32[1152,64]{0,1:T(8,128)}, u32[]{:S(2)}) copy-start(f32[1152,64]{0,1:T(8,128)} %param.20) | copy-start | bytes 884740
  7.2 163.3 %all-gather.6.cloned.1.call-start = ((), (), s32[]{:S(2)}) async-start(), calls=%async_computation.3 | async-start | bytes 2985984 | tf_op jit(solution)/shard_map/all_gather | solution.py:259
  7.9 9.3 %copy-start.6 = (s32[64,512]{1,0:T(8,128)S(1)}, s32[64,512]{1,0:T(8,128)}, u32[]{:S(2)}) copy-start(s32[64,512]{1,0:T(8,128)} %param.14) | copy-start | bytes 393220
  7.9 169.5 %all-gather.8.cloned.1.call-start = ((), (), s32[]{:S(2)}) async-start(), calls=%async_computation.4 | async-start | bytes 2985984 | tf_op jit(solution)/shard_map/all_gather | solution.py:259
  8.7 8.5 %copy-start.9 = (f32[2,144]{1,0:T(2,128)S(1)}, f32[2,144]{1,0:T(2,128)}, u32[]{:S(2)}) copy-start(f32[2,144]{1,0:T(2,128)} %param.15) | copy-start | bytes 3460
  8.7 176.2 %all-gather.10.cloned.1.call-start = ((), (), s32[]{:S(2)}) async-start(), calls=%async_computation.5 | async-start | bytes 2985984 | tf_op jit(solution)/shard_map/all_gather | solution.py:259
  12.5 15.2 %collective-permute-start = (bf16[4,144,512]{2,1,0:T(8,128)(2,1)S(1)}, bf16[4,144,512]{2,1,0:T(8,128)(2,1)S(1)}, u32[]{:S(2)}, u32[]{:S(2)}) collective-permute-start(bf16[4,144,512]{2,1,0:T(8,128)(2,1)S(1)} %bitcast.50), channel_id=1, source_target_pairs={{0,8},{8,16},{16,24},{1,9},{9,17},{17,25},{2,10},{10,18},{18,26},{... | collective-permute-start | bytes 1769480 | tf_op jit(solution)/shard_map/ppermute | solution.py:257
  15.9 15.8 %collective-permute-start.1 = (bf16[4,144,512]{2,1,0:T(8,128)(2,1)S(1)}, bf16[4,144,512]{2,1,0:T(8,128)(2,1)S(1)}, u32[]{:S(2)}, u32[]{:S(2)}) collective-permute-start(bf16[4,144,512]{2,1,0:T(8,128)(2,1)S(1)} %bitcast.51), channel_id=1, source_target_pairs={{8,0},{16,8},{24,16},{9,1},{17,9},{25,17},{10,2},{18,10},{26,18},{... | collective-permute-start | bytes 1769480 | tf_op jit(solution)/shard_map/ppermute | solution.py:258
  27.7 4.0 %copy-start.3 = (bf16[4,144,512]{2,1,0:T(8,128)(2,1)}, bf16[4,144,512]{2,1,0:T(8,128)(2,1)S(1)}, u32[]{:S(2)}) copy-start(bf16[4,144,512]{2,1,0:T(8,128)(2,1)S(1)} %collective-permute-done.up_ref) | copy-start | bytes 1769476
  31.7 0.8 copy-start.4
  78.0 61.2 %all-to-all-start.1 = ((f16[8,64,1024]{2,1,0:T(8,128)(2,1)}), f16[8,64,1024]{2,1,0:T(8,128)(2,1)S(1)}, u32[]{:S(2)}, u32[]{:S(2)}) async-start(f16[8,64,1024]{2,1,0:T(8,128)(2,1)} %convert_element_type.53), calls=%async_computation.1 | async-start | bytes 2097152 | tf_op jit(solution)/shard_map/all_to_all | solution.py:267
  83.7 108.9 %all-gather.12.cloned.1.call-start = ((), (), s32[]{:S(2)}) async-start(), calls=%async_computation.6 | async-start | bytes 2985984 | tf_op jit(solution)/shard_map/all_gather | solution.py:259
  163.6 6.9 %copy-start.5 = (bf16[1152,1024]{1,0:T(8,128)(2,1)}, bf16[1152,1024]{1,0:T(8,128)(2,1)S(1)}, u32[]{:S(2)}) copy-start(bf16[1152,1024]{1,0:T(8,128)(2,1)S(1)} %get-tuple-element.4) | copy-start | bytes 7077892
  184.9 7.7 %copy-start.2 = (bf16[1024,1152]{1,0:T(8,128)(2,1)}, bf16[1024,1152]{1,0:T(8,128)(2,1)S(1)}, u32[]{:S(2)}) copy-start(bf16[1024,1152]{1,0:T(8,128)(2,1)S(1)} %fusion.4) | copy-start | bytes 7077892
  206.0 52.4 %all-to-all-start.2 = ((bf16[8,144,1024]{2,1,0:T(8,128)(2,1)}), bf16[8,144,1024]{2,1,0:T(8,128)(2,1)}, u32[]{:S(2)}, u32[]{:S(2)}) async-start(bf16[8,144,1024]{2,1,0:T(8,128)(2,1)} %bitcast.46), calls=%async_computation.2 | async-start | bytes 4718592 | tf_op jit(solution)/shard_map/all_to_all | solution.py:280
  211.9 35.8 %all-gather.14.cloned.1.call-start = ((), (), s32[]{:S(2)}) async-start(), calls=%async_computation.7 | async-start | bytes 1179648 | tf_op jit(solution)/shard_map/all_gather | solution.py:279
  212.0 9.2 %copy-start.7 = (s32[1,1,2,2048]{3,2,1,0:T(2,128)S(1)}, s32[1,1,2,2048]{3,2,1,0:T(2,128)}, u32[]{:S(2)}) copy-start(s32[1,1,2,2048]{3,2,1,0:T(2,128)} %param.23) | copy-start | bytes 49156
  212.0 12.0 %copy-start.8 = (s32[1,1,2048]{2,1,0:T(1,128)S(1)}, s32[1,1,2048]{2,1,0:T(1,128)}, u32[]{:S(2)}) copy-start(s32[1,1,2048]{2,1,0:T(1,128)} %param.21) | copy-start | bytes 24580
  221.2 5.4 %copy-start.1 = (f32[8,80,1024]{2,1,0:T(8,128)S(1)}, f32[8,80,1024]{2,1,0:T(8,128)}, u32[]{:S(2)}) copy-start(f32[8,80,1024]{2,1,0:T(8,128)} %advect.2) | copy-start | bytes 7864324
Sparse Core Ops, SparseCore 0:
  9.9 31.7 all-gather.5
  43.5 30.5 all-gather.7
  76.0 38.5 all-gather.9
  116.3 30.1 all-gather.11
  221.3 26.3 all-gather.13
